TPU v7x, 1024 devices: a whole 4x8x16 slice. The times are simulated.
1024 devices in a mesh: seq: 64 (over y_hi, z), row: 2 (over core), col: 8 (over x, y_lo).
Axes of the slice: x: 4, y: 8 (y_hi: 4, y_lo: 2; y = y_hi * 2 + y_lo), z: 16, core: 2. Of those that a mesh axis runs over, the one named last changes fastest.
Arguments:
- tokens: bfloat16 [8192, 4096], P('seq', 'row'), may hold values from -40 to 40
- block_order: int32 [128], replicated, may hold values from 0 to 127, as said below
- query_weight: bfloat16 [4096, 4096], P('row', 'col'), may hold values from -0.09375 to 0.09375
- key_weight: bfloat16 [4096, 1024], P('row', 'col'), may hold values from -0.09375 to 0.09375
- value_weight: bfloat16 [4096, 1024], P('row', 'col'), may hold values from -0.09375 to 0.09375
- output_weight: bfloat16 [4096, 4096], P('col'), may hold values from -0.09375 to 0.09375
Outputs:
- layer_out: float32 [8192, 4096], P('seq', ('row', 'col'))
Inputs may be any that keep to these rules, and one draw needn't show every extreme that they name: Slots 2 d and 2 d + 1 are the rows of device d along seq; for every d, block_order[2 d + 1] = 127 - block_order[2 d] with block_order[2 d] < 64, and every half-block appears once.
All inputs are finite; a program needn't handle non-finite values.
Results may differ from a plain program's by a relative error of at most 0.012.
The roundings to bfloat16 on the way count: a program that leaves them out, or rounds other values in their place, can miss the bound.
Values may be sent and summed in bfloat16 or wider, within the bound.
No kernel may reach another device: no remote copies, remote signals or barrier semaphores. Data moves between devices by JAX's collectives and lax.ppermute only.
A program may use at most 32 MiB of HBM per device.

v0:
```python
from functools import partial

import jax
import jax.numpy as jnp
from jax import lax
from jax.sharding import PartitionSpec as P

HD = 128


rope_theta = 500000.0
large_negative = -1e30


def shifted(array, axis, by):
    peers = lax.axis_size(axis)
    return lax.ppermute(array, axis, [(i, (i + by) % peers) for i in range(peers)])


def rotate(vectors, positions):
    half_width = vectors.shape[-1] // 2
    freqs = rope_theta ** (-(jnp.arange(half_width, dtype=jnp.float32) * 2.0 / vectors.shape[-1]))
    angles = positions.astype(jnp.float32)[:, None] * freqs[None, :]
    cosine = jnp.cos(angles)[:, None, :]
    sine = jnp.sin(angles)[:, None, :]
    first = vectors[..., :half_width]
    second = vectors[..., half_width:]
    return jnp.concatenate(
        [first * cosine - second * sine, second * cosine + first * sine], axis=-1
    )


def token_positions(block_order, first_row, count, half_rows):
    rows_index = first_row + jnp.arange(count, dtype=jnp.int32)
    slots = rows_index // half_rows
    matched = slots[:, None] == jnp.arange(block_order.shape[0], dtype=jnp.int32)[None, :]
    chosen = jnp.sum(jnp.where(matched, block_order[None, :], 0), axis=1)
    return chosen * half_rows + rows_index % half_rows


def attend_block(queries, query_pos, carry_state, key_values, key_pos):
    highest, denom, accum = carry_state
    scores = jnp.einsum("qhd,kd->qhk", queries, key_values[0], preferred_element_type=jnp.float32)
    scores = scores * queries.shape[-1] ** (-0.5)
    visible = key_pos[None, None, :] <= query_pos[:, None, None]
    scores = jnp.where(visible, scores, large_negative)
    new_highest = jnp.maximum(highest, jnp.max(scores, axis=-1))
    rescale = jnp.exp(highest - new_highest)
    weights = jnp.where(visible, jnp.exp(scores - new_highest[..., None]), 0.0)
    denom = denom * rescale + jnp.sum(weights, axis=-1)
    mixed = jnp.einsum(
        "qhk,kd->qhd",
        weights.astype(jnp.bfloat16),
        key_values[1],
        preferred_element_type=jnp.float32,
    )
    accum = accum * rescale[..., None] + mixed
    return (new_highest, denom, accum)


def body(tokens, block_order, query_weight, key_weight, value_weight, output_weight):
    rows_here = tokens.shape[0]
    half_rows = rows_here // 2
    seq_count = lax.axis_size("seq")
    seq_index = lax.axis_index("seq")
    row_index = lax.axis_index("row")
    head_width = HD
    query_part = jnp.dot(tokens, query_weight, preferred_element_type=jnp.float32)
    queries = lax.psum_scatter(query_part, "row", scatter_dimension=1, tiled=True)
    keys_part = jnp.dot(tokens, key_weight, preferred_element_type=jnp.float32)
    values_part = jnp.dot(tokens, value_weight, preferred_element_type=jnp.float32)
    keys_summed, values_summed = lax.psum((keys_part, values_part), "row")
    heads_here = queries.shape[1] // head_width
    own_pos = token_positions(block_order, seq_index * rows_here, rows_here, half_rows)
    queries = rotate(queries.reshape(rows_here, heads_here, head_width), own_pos).astype(
        jnp.bfloat16
    )
    attend = partial(attend_block, queries, own_pos)
    carry_state = (
        jnp.full((rows_here, heads_here), large_negative, jnp.float32),
        jnp.zeros((rows_here, heads_here), jnp.float32),
        jnp.zeros((rows_here, heads_here, head_width), jnp.float32),
    )

    def source_positions(source):
        return token_positions(block_order, source * rows_here, rows_here, half_rows)

    key_one = keys_summed
    key_one = rotate(key_one[:, None, :], own_pos)[:, 0, :].astype(jnp.bfloat16)
    key_values = jnp.stack([key_one, values_summed.astype(jnp.bfloat16)])
    carry_state = attend(carry_state, key_values, own_pos)

    def beside_all(shift_count, loop_carry):
        carry_now, travelling = loop_carry
        travelling = shifted(travelling, "seq", 1)
        source = (seq_index - shift_count) % seq_count
        carry_now = attend(carry_now, travelling, source_positions(source))
        return (carry_now, travelling)

    carry_state, unused = lax.fori_loop(1, seq_count, beside_all, (carry_state, key_values))
    highest, denom, accum = carry_state
    attended = (
        (accum / denom[..., None]).astype(jnp.bfloat16).reshape(rows_here, heads_here * head_width)
    )
    out_rows = lax.dynamic_slice_in_dim(
        output_weight, row_index * heads_here * head_width, heads_here * head_width, 0
    )
    partial_out = jnp.dot(attended, out_rows, preferred_element_type=jnp.float32)
    return lax.psum_scatter(partial_out, ("row", "col"), scatter_dimension=1, tiled=True)


def solution(mesh):
    placed = (
        P("seq", "row"),
        P(),
        P("row", "col"),
        P("row", "col"),
        P("row", "col"),
        P("col", None),
    )
    return jax.shard_map(
        body, mesh=mesh, in_specs=placed, out_specs=P("seq", ("row", "col")), check_vma=False
    )
```

profile of v0, /device:TPU:1, one launch (start us, length us, event | category | flops | bytes accessed | tf_op | source)
XLA Modules:
  0.0 900.6 jit_solution(1116841227767856886)
XLA Ops:
  12.2 17.6 %psum.15 = bf16[128,128]{1,0:T(8,128)(2,1)S(1)} all-reduce(f32[128,128]{1,0:T(8,128)S(1)} %fusion.38), channel_id=1, replica_groups=mesh['seq'=64,'row'=2,'col'=8] {'row'}, use_global_device_ids=true, to_apply=%region_5.6 | all-reduce | flops 16384 | bytes 98304 | tf_op jit(solution)/shard_map/psum | solution.py:72
  29.7 37.5 %all-reduce.2.cloned.1.call-done = f32[128,1,128]{2,0,1:T(8,128)} async-done(((f32[128,1,128]{2,0,1:T(8,128)}), f32[128,1,128]{2,0,1:T(8,128)}) %all-reduce.2.cloned.1.call-update) | async-done | bytes 65552 | tf_op jit(solution)/shard_map/psum | solution.py:72
  68.6 24.8 %reduce-scatter.3.cloned.1.call-done = f32[128,256]{1,0:T(8,128)} async-done(((f32[128,512]{1,0:T(8,128)}), f32[128,256]{1,0:T(8,128)}) %reduce-scatter.3.cloned.1.call-update) | async-done | bytes 131088 | tf_op jit(solution)/shard_map/reduce_scatter | solution.py:69
  95.3 647.8 %while.21 = (s32[]{:T(128)}, f32[128,2]{0,1:T(2,128)S(1)}, f32[128,2]{0,1:T(2,128)S(1)}, f32[128,2,128]{2,0,1:T(8,128)S(1)}, bf16[2,128,128]{2,1,0:T(8,128)(2,1)...) while((s32[]{:T(128)}, f32[128,2]{0,1:T(2,128)S(1)}, ...), condition=%wide.region_10.11_spmd, body=%wide.region_6.10_spmd.sunk | while | flops 17207440 | bytes 1265978 | solution.py:100
  97.5 8.0 collective-permute-done
  108.3 7.5 collective-permute-done
  157.8 7.6 collective-permute-done
  168.2 7.7 collective-permute-done
  178.6 7.8 collective-permute-done
  189.3 7.7 collective-permute-done
  199.8 7.5 collective-permute-done
  210.1 7.7 collective-permute-done
  220.6 8.2 collective-permute-done
  231.5 7.7 collective-permute-done
  242.1 8.0 collective-permute-done
  252.8 7.6 collective-permute-done
  263.2 7.5 collective-permute-done
  273.5 7.5 collective-permute-done
  283.7 7.4 collective-permute-done
  293.9 7.5 collective-permute-done
  333.7 8.0 collective-permute-done
  344.5 8.3 collective-permute-done
  355.6 7.5 collective-permute-done
  385.6 7.6 collective-permute-done
  396.0 7.7 collective-permute-done
  406.5 7.7 collective-permute-done
  416.9 7.7 collective-permute-done
  427.4 7.6 collective-permute-done
  437.8 8.2 collective-permute-done
  448.8 8.6 collective-permute-done
  460.2 8.7 collective-permute-done
  481.4 7.2 collective-permute-done
  491.5 7.2 collective-permute-done
  501.5 7.2 collective-permute-done
  511.5 7.2 collective-permute-done
  521.5 7.2 collective-permute-done
  531.5 7.5 collective-permute-done
  541.8 8.5 collective-permute-done
  553.0 7.7 collective-permute-done
  593.1 7.4 collective-permute-done
  613.1 7.2 collective-permute-done
  623.1 7.6 collective-permute-done
  633.5 8.3 collective-permute-done
  654.6 7.2 collective-permute-done
  664.6 7.2 collective-permute-done
  714.5 8.2 collective-permute-done
  725.5 7.3 collective-permute-done
  746.6 147.4 %reduce-scatter.5.cloned.1.call-done = f32[128,256]{1,0:T(8,128)} async-done(((f32[128,4096]{1,0:T(8,128)}), f32[128,256]{1,0:T(8,128)}) %reduce-scatter.5.cloned.1.call-update) | async-done | bytes 131088 | tf_op jit(solution)/shard_map/reduce_scatter | solution.py:109
  (814 shorter events, 323.5 us)
Async XLA Ops:
  6.5 60.7 %all-reduce.2.cloned.1.call-start = ((), (), s32[]{:S(2)}) async-start(), calls=%async_computation.3 | async-start | bytes 131072 | tf_op jit(solution)/shard_map/psum | solution.py:72
  8.9 84.5 %reduce-scatter.3.cloned.1.call-start = ((), (), s32[]{:S(2)}) async-start(), calls=%async_computation.2 | async-start | bytes 393216 | tf_op jit(solution)/shard_map/reduce_scatter | solution.py:69
  11.2 882.9 %reduce-scatter.5.cloned.1.call-start = ((), (), s32[]{:S(2)}) async-start(), calls=%async_computation.4 | async-start | bytes 2228224 | tf_op jit(solution)/shard_map/reduce_scatter | solution.py:109
  95.3 10.3 %collective-permute-start = (bf16[2,128,128]{2,1,0:T(8,128)(2,1)S(1)}, bf16[2,128,128]{2,1,0:T(8,128)(2,1)S(1)}, u32[]{:S(2)}, u32[]{:S(2)}) collective-permute-start(bf16[2,128,128]{2,1,0:T(8,128)(2,1)S(1)} %get-tuple-element.348), channel_id=1, source_target_pairs={{0,16},{16,32},{32,48},{48,64},{64,80},{80,96},{96,112},{112,128},... | collective-permute-start | bytes 196616 | tf_op jit(solution)/shard_map/while/body/eval_jaxpr/ppermute | solution.py:17
  106.1 9.8 %collective-permute-start = (bf16[2,128,128]{2,1,0:T(8,128)(2,1)S(1)}, bf16[2,128,128]{2,1,0:T(8,128)(2,1)S(1)}, u32[]{:S(2)}, u32[]{:S(2)}) collective-permute-start(bf16[2,128,128]{2,1,0:T(8,128)(2,1)S(1)} %get-tuple-element.348), channel_id=1, source_target_pairs={{0,16},{16,32},{32,48},{48,64},{64,80},{80,96},{96,112},{112,128},... | collective-permute-start | bytes 196616 | tf_op jit(solution)/shard_map/while/body/eval_jaxpr/ppermute | solution.py:17
  155.5 9.9 %collective-permute-start = (bf16[2,128,128]{2,1,0:T(8,128)(2,1)S(1)}, bf16[2,128,128]{2,1,0:T(8,128)(2,1)S(1)}, u32[]{:S(2)}, u32[]{:S(2)}) collective-permute-start(bf16[2,128,128]{2,1,0:T(8,128)(2,1)S(1)} %get-tuple-element.348), channel_id=1, source_target_pairs={{0,16},{16,32},{32,48},{48,64},{64,80},{80,96},{96,112},{112,128},... | collective-permute-start | bytes 196616 | tf_op jit(solution)/shard_map/while/body/eval_jaxpr/ppermute | solution.py:17
  165.9 9.9 %collective-permute-start = (bf16[2,128,128]{2,1,0:T(8,128)(2,1)S(1)}, bf16[2,128,128]{2,1,0:T(8,128)(2,1)S(1)}, u32[]{:S(2)}, u32[]{:S(2)}) collective-permute-start(bf16[2,128,128]{2,1,0:T(8,128)(2,1)S(1)} %get-tuple-element.348), channel_id=1, source_target_pairs={{0,16},{16,32},{32,48},{48,64},{64,80},{80,96},{96,112},{112,128},... | collective-permute-start | bytes 196616 | tf_op jit(solution)/shard_map/while/body/eval_jaxpr/ppermute | solution.py:17
  176.4 10.1 %collective-permute-start = (bf16[2,128,128]{2,1,0:T(8,128)(2,1)S(1)}, bf16[2,128,128]{2,1,0:T(8,128)(2,1)S(1)}, u32[]{:S(2)}, u32[]{:S(2)}) collective-permute-start(bf16[2,128,128]{2,1,0:T(8,128)(2,1)S(1)} %get-tuple-element.348), channel_id=1, source_target_pairs={{0,16},{16,32},{32,48},{48,64},{64,80},{80,96},{96,112},{112,128},... | collective-permute-start | bytes 196616 | tf_op jit(solution)/shard_map/while/body/eval_jaxpr/ppermute | solution.py:17
  187.0 10.0 %collective-permute-start = (bf16[2,128,128]{2,1,0:T(8,128)(2,1)S(1)}, bf16[2,128,128]{2,1,0:T(8,128)(2,1)S(1)}, u32[]{:S(2)}, u32[]{:S(2)}) collective-permute-start(bf16[2,128,128]{2,1,0:T(8,128)(2,1)S(1)} %get-tuple-element.348), channel_id=1, source_target_pairs={{0,16},{16,32},{32,48},{48,64},{64,80},{80,96},{96,112},{112,128},... | collective-permute-start | bytes 196616 | tf_op jit(solution)/shard_map/while/body/eval_jaxpr/ppermute | solution.py:17
  197.5 9.8 %collective-permute-start = (bf16[2,128,128]{2,1,0:T(8,128)(2,1)S(1)}, bf16[2,128,128]{2,1,0:T(8,128)(2,1)S(1)}, u32[]{:S(2)}, u32[]{:S(2)}) collective-permute-start(bf16[2,128,128]{2,1,0:T(8,128)(2,1)S(1)} %get-tuple-element.348), channel_id=1, source_target_pairs={{0,16},{16,32},{32,48},{48,64},{64,80},{80,96},{96,112},{112,128},... | collective-permute-start | bytes 196616 | tf_op jit(solution)/shard_map/while/body/eval_jaxpr/ppermute | solution.py:17
  207.9 9.9 %collective-permute-start = (bf16[2,128,128]{2,1,0:T(8,128)(2,1)S(1)}, bf16[2,128,128]{2,1,0:T(8,128)(2,1)S(1)}, u32[]{:S(2)}, u32[]{:S(2)}) collective-permute-start(bf16[2,128,128]{2,1,0:T(8,128)(2,1)S(1)} %get-tuple-element.348), channel_id=1, source_target_pairs={{0,16},{16,32},{32,48},{48,64},{64,80},{80,96},{96,112},{112,128},... | collective-permute-start | bytes 196616 | tf_op jit(solution)/shard_map/while/body/eval_jaxpr/ppermute | solution.py:17
  218.3 10.4 %collective-permute-start = (bf16[2,128,128]{2,1,0:T(8,128)(2,1)S(1)}, bf16[2,128,128]{2,1,0:T(8,128)(2,1)S(1)}, u32[]{:S(2)}, u32[]{:S(2)}) collective-permute-start(bf16[2,128,128]{2,1,0:T(8,128)(2,1)S(1)} %get-tuple-element.348), channel_id=1, source_target_pairs={{0,16},{16,32},{32,48},{48,64},{64,80},{80,96},{96,112},{112,128},... | collective-permute-start | bytes 196616 | tf_op jit(solution)/shard_map/while/body/eval_jaxpr/ppermute | solution.py:17
  229.3 10.0 %collective-permute-start = (bf16[2,128,128]{2,1,0:T(8,128)(2,1)S(1)}, bf16[2,128,128]{2,1,0:T(8,128)(2,1)S(1)}, u32[]{:S(2)}, u32[]{:S(2)}) collective-permute-start(bf16[2,128,128]{2,1,0:T(8,128)(2,1)S(1)} %get-tuple-element.348), channel_id=1, source_target_pairs={{0,16},{16,32},{32,48},{48,64},{64,80},{80,96},{96,112},{112,128},... | collective-permute-start | bytes 196616 | tf_op jit(solution)/shard_map/while/body/eval_jaxpr/ppermute | solution.py:17
  239.8 10.2 %collective-permute-start = (bf16[2,128,128]{2,1,0:T(8,128)(2,1)S(1)}, bf16[2,128,128]{2,1,0:T(8,128)(2,1)S(1)}, u32[]{:S(2)}, u32[]{:S(2)}) collective-permute-start(bf16[2,128,128]{2,1,0:T(8,128)(2,1)S(1)} %get-tuple-element.348), channel_id=1, source_target_pairs={{0,16},{16,32},{32,48},{48,64},{64,80},{80,96},{96,112},{112,128},... | collective-permute-start | bytes 196616 | tf_op jit(solution)/shard_map/while/body/eval_jaxpr/ppermute | solution.py:17
  250.6 9.8 %collective-permute-start = (bf16[2,128,128]{2,1,0:T(8,128)(2,1)S(1)}, bf16[2,128,128]{2,1,0:T(8,128)(2,1)S(1)}, u32[]{:S(2)}, u32[]{:S(2)}) collective-permute-start(bf16[2,128,128]{2,1,0:T(8,128)(2,1)S(1)} %get-tuple-element.348), channel_id=1, source_target_pairs={{0,16},{16,32},{32,48},{48,64},{64,80},{80,96},{96,112},{112,128},... | collective-permute-start | bytes 196616 | tf_op jit(solution)/shard_map/while/body/eval_jaxpr/ppermute | solution.py:17
  260.9 9.7 %collective-permute-start = (bf16[2,128,128]{2,1,0:T(8,128)(2,1)S(1)}, bf16[2,128,128]{2,1,0:T(8,128)(2,1)S(1)}, u32[]{:S(2)}, u32[]{:S(2)}) collective-permute-start(bf16[2,128,128]{2,1,0:T(8,128)(2,1)S(1)} %get-tuple-element.348), channel_id=1, source_target_pairs={{0,16},{16,32},{32,48},{48,64},{64,80},{80,96},{96,112},{112,128},... | collective-permute-start | bytes 196616 | tf_op jit(solution)/shard_map/while/body/eval_jaxpr/ppermute | solution.py:17
  271.2 9.7 %collective-permute-start = (bf16[2,128,128]{2,1,0:T(8,128)(2,1)S(1)}, bf16[2,128,128]{2,1,0:T(8,128)(2,1)S(1)}, u32[]{:S(2)}, u32[]{:S(2)}) collective-permute-start(bf16[2,128,128]{2,1,0:T(8,128)(2,1)S(1)} %get-tuple-element.348), channel_id=1, source_target_pairs={{0,16},{16,32},{32,48},{48,64},{64,80},{80,96},{96,112},{112,128},... | collective-permute-start | bytes 196616 | tf_op jit(solution)/shard_map/while/body/eval_jaxpr/ppermute | solution.py:17
  281.5 9.7 %collective-permute-start = (bf16[2,128,128]{2,1,0:T(8,128)(2,1)S(1)}, bf16[2,128,128]{2,1,0:T(8,128)(2,1)S(1)}, u32[]{:S(2)}, u32[]{:S(2)}) collective-permute-start(bf16[2,128,128]{2,1,0:T(8,128)(2,1)S(1)} %get-tuple-element.348), channel_id=1, source_target_pairs={{0,16},{16,32},{32,48},{48,64},{64,80},{80,96},{96,112},{112,128},... | collective-permute-start | bytes 196616 | tf_op jit(solution)/shard_map/while/body/eval_jaxpr/ppermute | solution.py:17
  291.7 9.8 %collective-permute-start = (bf16[2,128,128]{2,1,0:T(8,128)(2,1)S(1)}, bf16[2,128,128]{2,1,0:T(8,128)(2,1)S(1)}, u32[]{:S(2)}, u32[]{:S(2)}) collective-permute-start(bf16[2,128,128]{2,1,0:T(8,128)(2,1)S(1)} %get-tuple-element.348), channel_id=1, source_target_pairs={{0,16},{16,32},{32,48},{48,64},{64,80},{80,96},{96,112},{112,128},... | collective-permute-start | bytes 196616 | tf_op jit(solution)/shard_map/while/body/eval_jaxpr/ppermute | solution.py:17
  331.4 10.3 %collective-permute-start = (bf16[2,128,128]{2,1,0:T(8,128)(2,1)S(1)}, bf16[2,128,128]{2,1,0:T(8,128)(2,1)S(1)}, u32[]{:S(2)}, u32[]{:S(2)}) collective-permute-start(bf16[2,128,128]{2,1,0:T(8,128)(2,1)S(1)} %get-tuple-element.348), channel_id=1, source_target_pairs={{0,16},{16,32},{32,48},{48,64},{64,80},{80,96},{96,112},{112,128},... | collective-permute-start | bytes 196616 | tf_op jit(solution)/shard_map/while/body/eval_jaxpr/ppermute | solution.py:17
  342.2 10.6 %collective-permute-start = (bf16[2,128,128]{2,1,0:T(8,128)(2,1)S(1)}, bf16[2,128,128]{2,1,0:T(8,128)(2,1)S(1)}, u32[]{:S(2)}, u32[]{:S(2)}) collective-permute-start(bf16[2,128,128]{2,1,0:T(8,128)(2,1)S(1)} %get-tuple-element.348), channel_id=1, source_target_pairs={{0,16},{16,32},{32,48},{48,64},{64,80},{80,96},{96,112},{112,128},... | collective-permute-start | bytes 196616 | tf_op jit(solution)/shard_map/while/body/eval_jaxpr/ppermute | solution.py:17
  353.3 9.7 %collective-permute-start = (bf16[2,128,128]{2,1,0:T(8,128)(2,1)S(1)}, bf16[2,128,128]{2,1,0:T(8,128)(2,1)S(1)}, u32[]{:S(2)}, u32[]{:S(2)}) collective-permute-start(bf16[2,128,128]{2,1,0:T(8,128)(2,1)S(1)} %get-tuple-element.348), channel_id=1, source_target_pairs={{0,16},{16,32},{32,48},{48,64},{64,80},{80,96},{96,112},{112,128},... | collective-permute-start | bytes 196616 | tf_op jit(solution)/shard_map/while/body/eval_jaxpr/ppermute | solution.py:17
  383.3 9.9 %collective-permute-start = (bf16[2,128,128]{2,1,0:T(8,128)(2,1)S(1)}, bf16[2,128,128]{2,1,0:T(8,128)(2,1)S(1)}, u32[]{:S(2)}, u32[]{:S(2)}) collective-permute-start(bf16[2,128,128]{2,1,0:T(8,128)(2,1)S(1)} %get-tuple-element.348), channel_id=1, source_target_pairs={{0,16},{16,32},{32,48},{48,64},{64,80},{80,96},{96,112},{112,128},... | collective-permute-start | bytes 196616 | tf_op jit(solution)/shard_map/while/body/eval_jaxpr/ppermute | solution.py:17
  393.8 9.9 %collective-permute-start = (bf16[2,128,128]{2,1,0:T(8,128)(2,1)S(1)}, bf16[2,128,128]{2,1,0:T(8,128)(2,1)S(1)}, u32[]{:S(2)}, u32[]{:S(2)}) collective-permute-start(bf16[2,128,128]{2,1,0:T(8,128)(2,1)S(1)} %get-tuple-element.348), channel_id=1, source_target_pairs={{0,16},{16,32},{32,48},{48,64},{64,80},{80,96},{96,112},{112,128},... | collective-permute-start | bytes 196616 | tf_op jit(solution)/shard_map/while/body/eval_jaxpr/ppermute | solution.py:17
  404.2 9.9 %collective-permute-start = (bf16[2,128,128]{2,1,0:T(8,128)(2,1)S(1)}, bf16[2,128,128]{2,1,0:T(8,128)(2,1)S(1)}, u32[]{:S(2)}, u32[]{:S(2)}) collective-permute-start(bf16[2,128,128]{2,1,0:T(8,128)(2,1)S(1)} %get-tuple-element.348), channel_id=1, source_target_pairs={{0,16},{16,32},{32,48},{48,64},{64,80},{80,96},{96,112},{112,128},... | collective-permute-start | bytes 196616 | tf_op jit(solution)/shard_map/while/body/eval_jaxpr/ppermute | solution.py:17
  414.7 9.9 %collective-permute-start = (bf16[2,128,128]{2,1,0:T(8,128)(2,1)S(1)}, bf16[2,128,128]{2,1,0:T(8,128)(2,1)S(1)}, u32[]{:S(2)}, u32[]{:S(2)}) collective-permute-start(bf16[2,128,128]{2,1,0:T(8,128)(2,1)S(1)} %get-tuple-element.348), channel_id=1, source_target_pairs={{0,16},{16,32},{32,48},{48,64},{64,80},{80,96},{96,112},{112,128},... | collective-permute-start | bytes 196616 | tf_op jit(solution)/shard_map/while/body/eval_jaxpr/ppermute | solution.py:17
  425.1 9.9 %collective-permute-start = (bf16[2,128,128]{2,1,0:T(8,128)(2,1)S(1)}, bf16[2,128,128]{2,1,0:T(8,128)(2,1)S(1)}, u32[]{:S(2)}, u32[]{:S(2)}) collective-permute-start(bf16[2,128,128]{2,1,0:T(8,128)(2,1)S(1)} %get-tuple-element.348), channel_id=1, source_target_pairs={{0,16},{16,32},{32,48},{48,64},{64,80},{80,96},{96,112},{112,128},... | collective-permute-start | bytes 196616 | tf_op jit(solution)/shard_map/while/body/eval_jaxpr/ppermute | solution.py:17
  435.6 10.4 %collective-permute-start = (bf16[2,128,128]{2,1,0:T(8,128)(2,1)S(1)}, bf16[2,128,128]{2,1,0:T(8,128)(2,1)S(1)}, u32[]{:S(2)}, u32[]{:S(2)}) collective-permute-start(bf16[2,128,128]{2,1,0:T(8,128)(2,1)S(1)} %get-tuple-element.348), channel_id=1, source_target_pairs={{0,16},{16,32},{32,48},{48,64},{64,80},{80,96},{96,112},{112,128},... | collective-permute-start | bytes 196616 | tf_op jit(solution)/shard_map/while/body/eval_jaxpr/ppermute | solution.py:17
  446.5 10.9 %collective-permute-start = (bf16[2,128,128]{2,1,0:T(8,128)(2,1)S(1)}, bf16[2,128,128]{2,1,0:T(8,128)(2,1)S(1)}, u32[]{:S(2)}, u32[]{:S(2)}) collective-permute-start(bf16[2,128,128]{2,1,0:T(8,128)(2,1)S(1)} %get-tuple-element.348), channel_id=1, source_target_pairs={{0,16},{16,32},{32,48},{48,64},{64,80},{80,96},{96,112},{112,128},... | collective-permute-start | bytes 196616 | tf_op jit(solution)/shard_map/while/body/eval_jaxpr/ppermute | solution.py:17
  457.9 10.9 %collective-permute-start = (bf16[2,128,128]{2,1,0:T(8,128)(2,1)S(1)}, bf16[2,128,128]{2,1,0:T(8,128)(2,1)S(1)}, u32[]{:S(2)}, u32[]{:S(2)}) collective-permute-start(bf16[2,128,128]{2,1,0:T(8,128)(2,1)S(1)} %get-tuple-element.348), channel_id=1, source_target_pairs={{0,16},{16,32},{32,48},{48,64},{64,80},{80,96},{96,112},{112,128},... | collective-permute-start | bytes 196616 | tf_op jit(solution)/shard_map/while/body/eval_jaxpr/ppermute | solution.py:17
  479.2 9.5 %collective-permute-start = (bf16[2,128,128]{2,1,0:T(8,128)(2,1)S(1)}, bf16[2,128,128]{2,1,0:T(8,128)(2,1)S(1)}, u32[]{:S(2)}, u32[]{:S(2)}) collective-permute-start(bf16[2,128,128]{2,1,0:T(8,128)(2,1)S(1)} %get-tuple-element.348), channel_id=1, source_target_pairs={{0,16},{16,32},{32,48},{48,64},{64,80},{80,96},{96,112},{112,128},... | collective-permute-start | bytes 196616 | tf_op jit(solution)/shard_map/while/body/eval_jaxpr/ppermute | solution.py:17
  489.2 9.5 %collective-permute-start = (bf16[2,128,128]{2,1,0:T(8,128)(2,1)S(1)}, bf16[2,128,128]{2,1,0:T(8,128)(2,1)S(1)}, u32[]{:S(2)}, u32[]{:S(2)}) collective-permute-start(bf16[2,128,128]{2,1,0:T(8,128)(2,1)S(1)} %get-tuple-element.348), channel_id=1, source_target_pairs={{0,16},{16,32},{32,48},{48,64},{64,80},{80,96},{96,112},{112,128},... | collective-permute-start | bytes 196616 | tf_op jit(solution)/shard_map/while/body/eval_jaxpr/ppermute | solution.py:17
  499.2 9.5 %collective-permute-start = (bf16[2,128,128]{2,1,0:T(8,128)(2,1)S(1)}, bf16[2,128,128]{2,1,0:T(8,128)(2,1)S(1)}, u32[]{:S(2)}, u32[]{:S(2)}) collective-permute-start(bf16[2,128,128]{2,1,0:T(8,128)(2,1)S(1)} %get-tuple-element.348), channel_id=1, source_target_pairs={{0,16},{16,32},{32,48},{48,64},{64,80},{80,96},{96,112},{112,128},... | collective-permute-start | bytes 196616 | tf_op jit(solution)/shard_map/while/body/eval_jaxpr/ppermute | solution.py:17
  509.2 9.5 %collective-permute-start = (bf16[2,128,128]{2,1,0:T(8,128)(2,1)S(1)}, bf16[2,128,128]{2,1,0:T(8,128)(2,1)S(1)}, u32[]{:S(2)}, u32[]{:S(2)}) collective-permute-start(bf16[2,128,128]{2,1,0:T(8,128)(2,1)S(1)} %get-tuple-element.348), channel_id=1, source_target_pairs={{0,16},{16,32},{32,48},{48,64},{64,80},{80,96},{96,112},{112,128},... | collective-permute-start | bytes 196616 | tf_op jit(solution)/shard_map/while/body/eval_jaxpr/ppermute | solution.py:17
  519.2 9.5 %collective-permute-start = (bf16[2,128,128]{2,1,0:T(8,128)(2,1)S(1)}, bf16[2,128,128]{2,1,0:T(8,128)(2,1)S(1)}, u32[]{:S(2)}, u32[]{:S(2)}) collective-permute-start(bf16[2,128,128]{2,1,0:T(8,128)(2,1)S(1)} %get-tuple-element.348), channel_id=1, source_target_pairs={{0,16},{16,32},{32,48},{48,64},{64,80},{80,96},{96,112},{112,128},... | collective-permute-start | bytes 196616 | tf_op jit(solution)/shard_map/while/body/eval_jaxpr/ppermute | solution.py:17
  529.2 9.7 %collective-permute-start = (bf16[2,128,128]{2,1,0:T(8,128)(2,1)S(1)}, bf16[2,128,128]{2,1,0:T(8,128)(2,1)S(1)}, u32[]{:S(2)}, u32[]{:S(2)}) collective-permute-start(bf16[2,128,128]{2,1,0:T(8,128)(2,1)S(1)} %get-tuple-element.348), channel_id=1, source_target_pairs={{0,16},{16,32},{32,48},{48,64},{64,80},{80,96},{96,112},{112,128},... | collective-permute-start | bytes 196616 | tf_op jit(solution)/shard_map/while/body/eval_jaxpr/ppermute | solution.py:17
  539.5 10.7 %collective-permute-start = (bf16[2,128,128]{2,1,0:T(8,128)(2,1)S(1)}, bf16[2,128,128]{2,1,0:T(8,128)(2,1)S(1)}, u32[]{:S(2)}, u32[]{:S(2)}) collective-permute-start(bf16[2,128,128]{2,1,0:T(8,128)(2,1)S(1)} %get-tuple-element.348), channel_id=1, source_target_pairs={{0,16},{16,32},{32,48},{48,64},{64,80},{80,96},{96,112},{112,128},... | collective-permute-start | bytes 196616 | tf_op jit(solution)/shard_map/while/body/eval_jaxpr/ppermute | solution.py:17
  550.8 10.0 %collective-permute-start = (bf16[2,128,128]{2,1,0:T(8,128)(2,1)S(1)}, bf16[2,128,128]{2,1,0:T(8,128)(2,1)S(1)}, u32[]{:S(2)}, u32[]{:S(2)}) collective-permute-start(bf16[2,128,128]{2,1,0:T(8,128)(2,1)S(1)} %get-tuple-element.348), channel_id=1, source_target_pairs={{0,16},{16,32},{32,48},{48,64},{64,80},{80,96},{96,112},{112,128},... | collective-permute-start | bytes 196616 | tf_op jit(solution)/shard_map/while/body/eval_jaxpr/ppermute | solution.py:17
  590.9 9.7 %collective-permute-start = (bf16[2,128,128]{2,1,0:T(8,128)(2,1)S(1)}, bf16[2,128,128]{2,1,0:T(8,128)(2,1)S(1)}, u32[]{:S(2)}, u32[]{:S(2)}) collective-permute-start(bf16[2,128,128]{2,1,0:T(8,128)(2,1)S(1)} %get-tuple-element.348), channel_id=1, source_target_pairs={{0,16},{16,32},{32,48},{48,64},{64,80},{80,96},{96,112},{112,128},... | collective-permute-start | bytes 196616 | tf_op jit(solution)/shard_map/while/body/eval_jaxpr/ppermute | solution.py:17
  610.8 9.5 %collective-permute-start = (bf16[2,128,128]{2,1,0:T(8,128)(2,1)S(1)}, bf16[2,128,128]{2,1,0:T(8,128)(2,1)S(1)}, u32[]{:S(2)}, u32[]{:S(2)}) collective-permute-start(bf16[2,128,128]{2,1,0:T(8,128)(2,1)S(1)} %get-tuple-element.348), channel_id=1, source_target_pairs={{0,16},{16,32},{32,48},{48,64},{64,80},{80,96},{96,112},{112,128},... | collective-permute-start | bytes 196616 | tf_op jit(solution)/shard_map/while/body/eval_jaxpr/ppermute | solution.py:17
  620.8 9.9 %collective-permute-start = (bf16[2,128,128]{2,1,0:T(8,128)(2,1)S(1)}, bf16[2,128,128]{2,1,0:T(8,128)(2,1)S(1)}, u32[]{:S(2)}, u32[]{:S(2)}) collective-permute-start(bf16[2,128,128]{2,1,0:T(8,128)(2,1)S(1)} %get-tuple-element.348), channel_id=1, source_target_pairs={{0,16},{16,32},{32,48},{48,64},{64,80},{80,96},{96,112},{112,128},... | collective-permute-start | bytes 196616 | tf_op jit(solution)/shard_map/while/body/eval_jaxpr/ppermute | solution.py:17
  631.3 10.6 %collective-permute-start = (bf16[2,128,128]{2,1,0:T(8,128)(2,1)S(1)}, bf16[2,128,128]{2,1,0:T(8,128)(2,1)S(1)}, u32[]{:S(2)}, u32[]{:S(2)}) collective-permute-start(bf16[2,128,128]{2,1,0:T(8,128)(2,1)S(1)} %get-tuple-element.348), channel_id=1, source_target_pairs={{0,16},{16,32},{32,48},{48,64},{64,80},{80,96},{96,112},{112,128},... | collective-permute-start | bytes 196616 | tf_op jit(solution)/shard_map/while/body/eval_jaxpr/ppermute | solution.py:17
  652.4 9.5 %collective-permute-start = (bf16[2,128,128]{2,1,0:T(8,128)(2,1)S(1)}, bf16[2,128,128]{2,1,0:T(8,128)(2,1)S(1)}, u32[]{:S(2)}, u32[]{:S(2)}) collective-permute-start(bf16[2,128,128]{2,1,0:T(8,128)(2,1)S(1)} %get-tuple-element.348), channel_id=1, source_target_pairs={{0,16},{16,32},{32,48},{48,64},{64,80},{80,96},{96,112},{112,128},... | collective-permute-start | bytes 196616 | tf_op jit(solution)/shard_map/while/body/eval_jaxpr/ppermute | solution.py:17
  662.4 9.5 %collective-permute-start = (bf16[2,128,128]{2,1,0:T(8,128)(2,1)S(1)}, bf16[2,128,128]{2,1,0:T(8,128)(2,1)S(1)}, u32[]{:S(2)}, u32[]{:S(2)}) collective-permute-start(bf16[2,128,128]{2,1,0:T(8,128)(2,1)S(1)} %get-tuple-element.348), channel_id=1, source_target_pairs={{0,16},{16,32},{32,48},{48,64},{64,80},{80,96},{96,112},{112,128},... | collective-permute-start | bytes 196616 | tf_op jit(solution)/shard_map/while/body/eval_jaxpr/ppermute | solution.py:17
  672.4 9.5 %collective-permute-start = (bf16[2,128,128]{2,1,0:T(8,128)(2,1)S(1)}, bf16[2,128,128]{2,1,0:T(8,128)(2,1)S(1)}, u32[]{:S(2)}, u32[]{:S(2)}) collective-permute-start(bf16[2,128,128]{2,1,0:T(8,128)(2,1)S(1)} %get-tuple-element.348), channel_id=1, source_target_pairs={{0,16},{16,32},{32,48},{48,64},{64,80},{80,96},{96,112},{112,128},... | collective-permute-start | bytes 196616 | tf_op jit(solution)/shard_map/while/body/eval_jaxpr/ppermute | solution.py:17
  682.4 9.5 %collective-permute-start = (bf16[2,128,128]{2,1,0:T(8,128)(2,1)S(1)}, bf16[2,128,128]{2,1,0:T(8,128)(2,1)S(1)}, u32[]{:S(2)}, u32[]{:S(2)}) collective-permute-start(bf16[2,128,128]{2,1,0:T(8,128)(2,1)S(1)} %get-tuple-element.348), channel_id=1, source_target_pairs={{0,16},{16,32},{32,48},{48,64},{64,80},{80,96},{96,112},{112,128},... | collective-permute-start | bytes 196616 | tf_op jit(solution)/shard_map/while/body/eval_jaxpr/ppermute | solution.py:17
  712.2 10.4 %collective-permute-start = (bf16[2,128,128]{2,1,0:T(8,128)(2,1)S(1)}, bf16[2,128,128]{2,1,0:T(8,128)(2,1)S(1)}, u32[]{:S(2)}, u32[]{:S(2)}) collective-permute-start(bf16[2,128,128]{2,1,0:T(8,128)(2,1)S(1)} %get-tuple-element.348), channel_id=1, source_target_pairs={{0,16},{16,32},{32,48},{48,64},{64,80},{80,96},{96,112},{112,128},... | collective-permute-start | bytes 196616 | tf_op jit(solution)/shard_map/while/body/eval_jaxpr/ppermute | solution.py:17
  723.2 9.5 %collective-permute-start = (bf16[2,128,128]{2,1,0:T(8,128)(2,1)S(1)}, bf16[2,128,128]{2,1,0:T(8,128)(2,1)S(1)}, u32[]{:S(2)}, u32[]{:S(2)}) collective-permute-start(bf16[2,128,128]{2,1,0:T(8,128)(2,1)S(1)} %get-tuple-element.348), channel_id=1, source_target_pairs={{0,16},{16,32},{32,48},{48,64},{64,80},{80,96},{96,112},{112,128},... | collective-permute-start | bytes 196616 | tf_op jit(solution)/shard_map/while/body/eval_jaxpr/ppermute | solution.py:17
  (22 other events, 184.4 us)
Sparse Core Ops, SparseCore 0:
  10.8 56.4 all-reduce.1
  70.6 22.7 reduce-scatter.2
  746.7 147.2 reduce-scatter.4
where the time goes:
time: 906 us; the launch traced here: 901 us
  waiting for transfers between devices  682 us (75%)
  starting transfers between devices  121 us (13%)
  matrix products  34.7 us (4%)
  other arithmetic  24.6 us (3%)
  blocking collectives  17.6 us (2%)
  between operations  13.3 us (1%)
    ppermute x63, waiting for transfers between devices, shifted(): lax.ppermute(array, axis, [(i, (i + by) % peers) for i in range(peers)])  472 us
    reduce_scatter x1, waiting for transfers between devices, body(): lax.psum_scatter(partial_out, ('row', 'col'), scatter_dimension=1, tiled=...  147 us
    ppermute x63, starting transfers between devices, shifted(): lax.ppermute(array, axis, [(i, (i + by) % peers) for i in range(peers)])  121 us
    psum x1, waiting for transfers between devices, body(): keys_summed, values_summed = lax.psum((keys_part, values_part), 'row')  37.5 us
    reduce_scatter x1, waiting for transfers between devices, body(): lax.psum_scatter(query_part, 'row', scatter_dimension=1, tiled=True)  24.8 us
  transfers between devices with their start and end apart: 66, of which 66 were waited for; matrix products, arithmetic and copies ran while one was open for 2% of the time, Pallas kernels for 0%

commit v1 on v0

v1 whole, which is shorter than its diff:
```python
from functools import partial

import jax
import jax.numpy as jnp
from jax import lax
from jax.experimental import pallas as pl
from jax.experimental.pallas import tpu as pltpu
from jax.sharding import Mesh, PartitionSpec as P

HD = 128
rope_theta = 500000.0
large_negative = -1e30
score_to_log2 = float(HD**-0.5 * 1.4426950408889634)
f32 = jnp.float32
bf16 = jnp.bfloat16
VMEM = pl.BlockSpec(memory_space=pltpu.VMEM)
SMEM = pl.BlockSpec(memory_space=pltpu.SMEM)
HBM = pl.BlockSpec(memory_space=pltpu.HBM)


def params(kib):
    return pltpu.CompilerParams(vmem_limit_bytes=kib * 1024)


def dot_t(a, b):
    return lax.dot_general(a, b, (((1,), (1,)), ((), ())), preferred_element_type=f32)


def place():
    return lax.axis_index("yh"), lax.axis_index("z"), lax.axis_index("row")


def project_kernel(
    peers, order_ref, freq_ref, tok_ref, qw_ref, kw_ref, vw_ref, own_ref, send_ref, angle_ref, tok, weight, acc, sems
):
    q_width = qw_ref.shape[1]
    depth = tok_ref.shape[1]
    chunks = sems.shape[0]
    blk = depth // chunks
    copies = []
    for c in range(chunks):
        at = slice(c * blk, (c + 1) * blk)
        pairs = (
            (tok_ref.at[:, at], tok.at[:, at]),
            (qw_ref.at[at], weight.at[at, :q_width]),
            (kw_ref.at[at], weight.at[at, q_width : q_width + HD]),
            (vw_ref.at[at], weight.at[at, q_width + HD :]),
        )
        copies.append([pltpu.make_async_copy(*pair, sems.at[c, k]) for k, pair in enumerate(pairs)])
        for copy in copies[-1]:
            copy.start()

    yh, z, row = place()
    half = acc.shape[0] // 2
    part = half // 2
    index = lax.broadcasted_iota(jnp.int32, angle_ref.shape, 0)
    slot = 2 * (yh * peers + z)
    block = jnp.where(index < part, order_ref[slot], order_ref[slot + 1])
    position = block * half + row * part + (index & (part - 1))
    angle_ref[...] = position.astype(f32) * freq_ref[...]

    for c in range(chunks):
        at = slice(c * blk, (c + 1) * blk)
        for copy in copies[c]:
            copy.wait()
        product = jnp.dot(tok[:, at], weight[at], preferred_element_type=f32)
        acc[...] = product if c == 0 else acc[...] + product

    for k in range(2):
        mine = pl.ds(pl.multiple_of(k * half + row * part, part), part)
        theirs = pl.ds(pl.multiple_of(k * half + (1 - row) * part, part), part)
        own_ref[k * part : (k + 1) * part, :] = acc[mine, :]
        send_ref[k * part : (k + 1) * part, :] = acc[theirs, :]


def project(order, freqs, tokens, query_weight, key_weight, value_weight):
    rows, depth = tokens.shape
    width = query_weight.shape[1] + 2 * HD
    chunks = 4
    out = jax.ShapeDtypeStruct((rows // 2, width), f32)
    return pl.pallas_call(
        partial(project_kernel, lax.axis_size("z")),
        in_specs=[SMEM, VMEM] + [HBM] * 4,
        out_specs=[VMEM] * 3,
        out_shape=[out, out, jax.ShapeDtypeStruct((rows // 2, HD), f32)],
        scratch_shapes=[
            pltpu.VMEM((rows, depth), bf16),
            pltpu.VMEM((depth, width), bf16),
            pltpu.VMEM((rows, width), f32),
            pltpu.SemaphoreType.DMA((chunks, 4)),
        ],
        compiler_params=params(60000),
        name="project",
    )(order, freqs, tokens, query_weight, key_weight, value_weight)


def rope_kernel(own_ref, recv_ref, cos_ref, sin_ref, q_ref, kv_ref):
    cosine = cos_ref[...]
    lane = lax.broadcasted_iota(jnp.int32, sin_ref.shape, 1)
    sine = jnp.where(lane < HD // 2, -sin_ref[...], sin_ref[...])
    heads = q_ref.shape[1] // HD
    for h in range(heads + 1):
        cols = slice(h * HD, (h + 1) * HD)
        x = own_ref[:, cols] + recv_ref[:, cols]
        y = (x * cosine + pltpu.roll(x, HD // 2, 1) * sine).astype(bf16)
        if h < heads:
            q_ref[:, cols] = y
        else:
            kv_ref[:, :HD] = y
    cols = slice((heads + 1) * HD, (heads + 2) * HD)
    kv_ref[:, HD:] = (own_ref[:, cols] + recv_ref[:, cols]).astype(bf16)


def attend_kernel(order_ref, q_ref, own_ref, other_ref, ow_hbm, out_ref, ow_ref, sem):
    fetch = pltpu.make_async_copy(ow_hbm, ow_ref, sem)
    fetch.start()
    yh, z, row = place()
    peers_a, tok, width = q_ref.shape
    peers_e = own_ref.shape[0]
    part = tok // 2
    heads = width // HD
    rows = heads * part
    keys = peers_e * part

    lane = lax.broadcasted_iota(jnp.int32, (1, keys), 1)
    low_base = jnp.zeros((1, keys), jnp.int32)
    high_base = jnp.zeros((1, keys), jnp.int32)
    for e in range(peers_e):
        at = (lane >= e * part) & (lane < (e + 1) * part)
        slot = 2 * (yh * peers_e + e)
        low_base = jnp.where(at, order_ref[slot], low_base)
        high_base = jnp.where(at, order_ref[slot + 1], high_base)
    inner = lane & (part - 1)

    def side(base, core):
        return base * (2 * part) + inner + core * part

    low_pos = jnp.concatenate([side(low_base, row), side(low_base, 1 - row)], axis=1)
    high_pos = jnp.concatenate([side(high_base, row), side(high_base, 1 - row)], axis=1)

    def both(first, last, c0):
        pieces = [
            ref[:, first:last, c0 : c0 + HD].reshape(keys, HD) for ref in (own_ref, other_ref)
        ]
        return jnp.concatenate(pieces, axis=0)

    k_low, v_low = both(0, part, 0), both(0, part, HD)
    k_high, v_high = both(part, tok, 0), both(part, tok, HD)
    q_inner = lax.broadcasted_iota(jnp.int32, (rows, 1), 0) & (part - 1)
    spot = lax.broadcasted_iota(jnp.int32, (rows, HD), 1)

    for a in range(peers_a):
        slot = 2 * (a * peers_e + z)

        def stacked(first, last):
            return jnp.concatenate(
                [q_ref[a, first:last, h * HD : (h + 1) * HD] for h in range(heads)], axis=0
            )

        q_low, q_high = stacked(0, part), stacked(part, tok)
        q_low_pos = order_ref[slot] * (2 * part) + row * part + q_inner
        q_high_pos = order_ref[slot + 1] * (2 * part) + row * part + q_inner

        s_ll = jnp.where(low_pos <= q_low_pos, dot_t(q_low, k_low), large_negative)
        m_low = jnp.maximum(jnp.max(s_ll, axis=1, keepdims=True), large_negative * 0.1)
        p_ll = jnp.exp2((s_ll - m_low) * score_to_log2)
        d_low = jnp.sum(p_ll, axis=1, keepdims=True)
        o_low = jnp.dot(p_ll.astype(bf16), v_low, preferred_element_type=f32)

        s_hl = dot_t(q_high, k_low)
        s_hh = jnp.where(high_pos <= q_high_pos, dot_t(q_high, k_high), large_negative)
        m_high = jnp.maximum(
            jnp.max(s_hl, axis=1, keepdims=True), jnp.max(s_hh, axis=1, keepdims=True)
        )
        p_hl = jnp.exp2((s_hl - m_high) * score_to_log2)
        p_hh = jnp.exp2((s_hh - m_high) * score_to_log2)
        d_high = jnp.sum(p_hl, axis=1, keepdims=True) + jnp.sum(p_hh, axis=1, keepdims=True)
        o_high = jnp.dot(p_hl.astype(bf16), v_low, preferred_element_type=f32) + jnp.dot(
            p_hh.astype(bf16), v_high, preferred_element_type=f32
        )

        logs = jnp.zeros((rows, HD), f32)
        for i, (m, d, o) in enumerate(((m_low, d_low, o_low), (m_high, d_high, o_high))):
            seen = d > 0.0
            safe = jnp.where(seen, d, 1.0)
            out_ref[a, i * rows : (i + 1) * rows, :] = (o / safe).astype(bf16)
            log = jnp.where(seen, m * score_to_log2 + jnp.log2(safe), large_negative)
            for j in range(3):
                piece = log.astype(bf16).astype(f32)
                logs = jnp.where(spot == 3 * i + j, piece, logs)
                log = log - piece
        out_ref[a, 2 * rows :, :] = logs.T[:16, :].astype(bf16)
    fetch.wait()


def output_kernel(parts_ref, ow_ref, out_ref, att):
    peers, _, _ = parts_ref.shape
    tok, width = att.shape
    part = tok // 2
    heads = width // HD
    rows = heads * part

    shares = []
    for i in range(2):
        logs = []
        for p in range(peers):
            got = parts_ref[p, 2 * rows : 2 * rows + 16, :].astype(f32)
            logs.append(got[3 * i : 3 * i + 1] + got[3 * i + 1 : 3 * i + 2] + got[3 * i + 2 : 3 * i + 3])
        top = logs[0]
        for log in logs[1:]:
            top = jnp.maximum(top, log)
        weights = [jnp.exp2(log - top) for log in logs]
        total = weights[0]
        for w in weights[1:]:
            total = total + w
        shares += [w / total for w in weights]
    filled = jnp.concatenate(shares + [jnp.zeros((HD - 2 * peers, rows), f32)], axis=0)
    columns = filled.T
    for i in range(2):
        joined = jnp.zeros((rows, HD), f32)
        for p in range(peers):
            at = i * peers + p
            got = parts_ref[p, i * rows : (i + 1) * rows, :].astype(f32)
            joined += columns[:, at : at + 1] * got
        joined = joined.astype(bf16)
        for h in range(heads):
            att[i * part : (i + 1) * part, h * HD : (h + 1) * HD] = joined[h * part : (h + 1) * part, :]

    size = out_ref.shape[2]
    for k in range(out_ref.shape[0]):
        cols = slice(k * size, (k + 1) * size)
        out_ref[k] = jnp.dot(att[...], ow_ref[:, cols], preferred_element_type=f32).astype(bf16)


def output(parts, output_weight, tok, peers):
    width, columns = output_weight.shape
    return pl.pallas_call(
        output_kernel,
        in_specs=[VMEM] * 2,
        out_specs=VMEM,
        out_shape=jax.ShapeDtypeStruct((peers, tok, columns // peers), bf16),
        scratch_shapes=[pltpu.VMEM((tok, width), bf16)],
        compiler_params=params(12288),
        name="output",
    )(parts, output_weight)


def gather_kernel(recv_ref, out_ref):
    part = recv_ref.shape[1] // 2
    peers = recv_ref.shape[0] // 2
    for core in range(2):
        total = recv_ref[core * peers].astype(f32)
        for c in range(1, peers):
            total = total + recv_ref[core * peers + c].astype(f32)
        for k in range(2):
            at = 2 * k * part + core * part
            out_ref[at : at + part, :] = total[k * part : (k + 1) * part, :]


def body(tokens, block_order, query_weight, key_weight, value_weight, output_weight):
    rows_here = tokens.shape[0]
    tok = rows_here // 2
    part = tok // 2
    q_width = query_weight.shape[1]

    half_width = HD // 2
    freqs = rope_theta ** (-(jnp.arange(half_width, dtype=f32) * 2.0 / HD))
    freqs = jnp.concatenate([freqs, freqs])[None]
    own, send, angles = project(block_order, freqs, tokens, query_weight, key_weight, value_weight)
    recv = lax.ppermute(send, "row", [(0, 1), (1, 0)])

    queries, key_values = pl.pallas_call(
        rope_kernel,
        in_specs=[VMEM] * 4,
        out_specs=[VMEM] * 2,
        out_shape=[
            jax.ShapeDtypeStruct((tok, q_width), bf16),
            jax.ShapeDtypeStruct((tok, 2 * HD), bf16),
        ],
        compiler_params=params(8192),
        name="rope",
    )(own, recv, jnp.cos(angles), jnp.sin(angles))

    peers_a = lax.axis_size("yh")
    spread = jnp.broadcast_to(queries[None], (peers_a, tok, q_width))
    all_queries = lax.all_to_all(spread, "yh", 0, 0)
    own_keys = lax.all_gather(key_values, "z")
    other_keys = lax.ppermute(own_keys, "row", [(0, 1), (1, 0)])

    heads = q_width // HD
    result, fetched = pl.pallas_call(
        attend_kernel,
        in_specs=[SMEM, VMEM, VMEM, VMEM, HBM],
        out_specs=[VMEM] * 2,
        out_shape=[
            jax.ShapeDtypeStruct((peers_a, 2 * heads * part + 16, HD), bf16),
            jax.ShapeDtypeStruct(output_weight.shape, bf16),
        ],
        scratch_shapes=[pltpu.SemaphoreType.DMA],
        compiler_params=params(48000),
        name="attend",
    )(block_order, all_queries, own_keys, other_keys, output_weight)

    parts = lax.all_to_all(result, "yh", 0, 0)
    across = ("row", "x", "yl")
    partial_out = output(parts, fetched, tok, lax.axis_size(across))
    shares = lax.all_to_all(partial_out, across, 0, 0)
    return pl.pallas_call(
        gather_kernel,
        in_specs=[VMEM],
        out_specs=VMEM,
        out_shape=jax.ShapeDtypeStruct((rows_here, shares.shape[2]), f32),
        compiler_params=params(8192),
        name="gather",
    )(shares)


def solution(mesh):
    seq, row, col = (mesh.shape[name] for name in ("seq", "row", "col"))
    z = min(16, seq // 2)
    yl = 2 if col == 8 else 1
    devices = mesh.devices.reshape(seq // z, z, row, col // yl, yl)
    fine = Mesh(devices, ("yh", "z", "row", "x", "yl"))
    seq_axes, col_axes = ("yh", "z"), ("x", "yl")
    placed = (
        P(seq_axes, "row"),
        P(),
        P("row", col_axes),
        P("row", col_axes),
        P("row", col_axes),
        P(col_axes, None),
    )
    return jax.shard_map(
        body,
        mesh=fine,
        in_specs=placed,
        out_specs=P(seq_axes, ("row", *col_axes)),
        check_vma=False,
    )
```

time: 906 us -> 111 us (0.12)
  waiting for transfers between devices: 682 us -> 0.37 us
  starting transfers between devices: 121 us -> 25.3 us
  blocking collectives: 17.6 us -> 71.5 us
  matrix products: 34.7 us -> 0 us
  other arithmetic: 24.6 us -> 0.68 us
  between operations: 13.3 us -> 0.06 us
  Pallas kernels: 0 us -> 10.3 us
    ppermute x63 -> x2, waiting for transfers between devices: 472 us -> 0.37 us  [the longest x1 0.37 us: body(): recv = lax.ppermute(send, 'row', [(0, 1), (1, 0)])]
    reduce_scatter x2 -> x0, waiting for transfers between devices: 172 us -> none  [the longest x1 147 us: body(): lax.psum_scatter(partial_out, ('row', 'col'), scatter_dimension=1, tiled=...]
    ppermute x63 -> x2, starting transfers between devices: 121 us -> 25.3 us  [the longest x1 16 us: body(): recv = lax.ppermute(send, 'row', [(0, 1), (1, 0)])]
    all_to_all x0 -> x3, blocking collectives: none -> 45.6 us  [the longest x1 16.6 us: body(): all_queries = lax.all_to_all(spread, 'yh', 0, 0)]
    psum x1 -> x0, waiting for transfers between devices: 37.5 us -> none  [body(): keys_summed, values_summed = lax.psum((keys_part, values_part), 'row')]
    dot_general x132 -> x0, matrix products: 34.7 us -> none  [the longest x64 14.5 us: attend_block(): jnp.einsum('qhk,kd->qhd', weights.astype(jnp.bfloat16), key_values[1], pr...]
    all_gather x0 -> x1, blocking collectives: none -> 25.9 us  [body(): own_keys = lax.all_gather(key_values, 'z')]
    psum x1 -> x0, blocking collectives: 17.6 us -> none  [body(): keys_summed, values_summed = lax.psum((keys_part, values_part), 'row')]
  transfers between devices with their start and end apart: 66 -> 2, of which waited for: 66 -> 1; matrix products, arithmetic and copies ran while one was open for 2% -> 1% of each run, Pallas kernels for 0% -> 0%
where the time goes in v1:
time: 111 us; the launch traced here: 110 us
  blocking collectives  71.5 us (64%)
  starting transfers between devices  25.3 us (23%)
  Pallas kernels  10.3 us (9%)
  local copies, waits for them, and re-layouts  1.84 us (2%)
    all_gather x1, blocking collectives, body(): own_keys = lax.all_gather(key_values, 'z')  25.9 us
    all_to_all x1, blocking collectives, body(): all_queries = lax.all_to_all(spread, 'yh', 0, 0)  16.6 us
    ppermute x1, starting transfers between devices, body(): recv = lax.ppermute(send, 'row', [(0, 1), (1, 0)])  16 us
    all_to_all x1, blocking collectives, body(): shares = lax.all_to_all(partial_out, across, 0, 0)  15.8 us
    all_to_all x1, blocking collectives, body(): parts = lax.all_to_all(result, 'yh', 0, 0)  13.3 us
    ppermute x1, starting transfers between devices, body(): other_keys = lax.ppermute(own_keys, 'row', [(0, 1), (1, 0)])  9.32 us
    pallas_call x1, Pallas kernels, body(): pl.pallas_call(attend_kernel, in_specs=[SMEM, VMEM, VMEM, VMEM, HBM], out...  4.42 us
    pallas_call x1, Pallas kernels, project(): pl.pallas_call(partial(project_kernel, lax.axis_size('z')), in_specs=[SME...  3.94 us
  transfers between devices with their start and end apart: 2, of which 1 were waited for; matrix products, arithmetic and copies ran while one was open for 1% of the time, Pallas kernels for 0%

profile of v1, /device:TPU:1, one launch (start us, length us, event | category | flops | bytes accessed | tf_op | source)
XLA Modules:
  0.0 110.2 jit_solution(7661971863607337428)
XLA Ops:
  0.0 0.0 copy-start.1
  0.0 0.7 maximum_bitcast_fusion.freq_ref
  0.7 3.9 %project.1 = (f32[64,768]{1,0:T(8,128)}, f32[64,768]{1,0:T(8,128)}, f32[64,128]{1,0:T(8,128)}) custom-call(s32[128]{0:T(128)} %order_ref.3, f32[1,128]{1,0:T(1,128)} %maximum_bitcast_fusion.freq_ref, bf16[128,2048]{1,0:T(8,128)(2,1)} %tok_ref.1, bf16[2048,512]{1,0:T(8,128)(2,1)} %qw_ref.1, bf16[2048,128]{1,0:T(8,128)(2,1)} %kw_ref.1, bf16[2048,128]{1,0:T(8,128)(2,1)} %vw_ref.1), custom_call_target="tpu_custom_call" | custom-call | tf_op jit(solution)/shard_map/project/pallas_call | solution.py:81
  4.6 16.0 %collective-permute-start = (f32[64,768]{1,0:T(8,128)}, f32[64,768]{1,0:T(8,128)S(1)}, u32[]{:S(2)}, u32[]{:S(2)}) collective-permute-start(f32[64,768]{1,0:T(8,128)} %get-tuple-element.13), channel_id=1, source_target_pairs={{0,8},{8,0},{1,9},{9,1},{2,10},{10,2},{3,11},{11,3},{4,12},{12,4},... | collective-permute-start | bytes 589832 | tf_op jit(solution)/shard_map/ppermute | solution.py:270
  20.7 0.9 fusion
  21.5 0.4 collective-permute-done.recv_ref
  21.9 0.0 copy-start
  21.9 0.9 copy-done
  22.8 0.1 rope.1
  23.0 25.9 %all-gather = bf16[1024,256]{1,0:T(8,128)(2,1)S(1)} all-gather(bf16[64,256]{1,0:T(8,128)(2,1)S(1)} %get-tuple-element.16), channel_id=2, replica_groups=mesh['yh'=4,'z'=16,'row'=2,'x'=4,'yl'=2] {'z'}, dimensions={0}, use_global_device_ids=true | all-gather | bytes 557056 | tf_op jit(solution)/shard_map/all_gather | solution.py:287
  48.9 9.3 %collective-permute-start.1 = (bf16[16,64,256]{2,1,0:T(8,128)(2,1)S(1)}, bf16[16,64,256]{2,1,0:T(8,128)(2,1)S(1)}, u32[]{:S(2)}, u32[]{:S(2)}) collective-permute-start(bf16[16,64,256]{2,1,0:T(8,128)(2,1)S(1)} %bitcast.3), channel_id=1, source_target_pairs={{0,8},{8,0},{1,9},{9,1},{2,10},{10,2},{3,11},{11,3},{4,12},{12,4},... | collective-permute-start | bytes 1572872 | tf_op jit(solution)/shard_map/ppermute | solution.py:288
  58.2 16.6 %all_to_all.15.q_ref = bf16[4,64,512]{2,1,0:T(8,128)(2,1)S(1)} all-to-all(bf16[4,64,512]{2,1,0:T(8,128)(2,1)S(1)} %broadcast_in_dim.10), channel_id=1, replica_groups=mesh['yh'=4,'z'=16,'row'=2,'x'=4,'yl'=2] {'yh'}, dimensions={0} | all-to-all | bytes 524288 | tf_op jit(solution)/shard_map/all_to_all | solution.py:286
  74.8 0.0 collective-permute-done.1.other_ref
  74.8 0.0 copy-done.1
  74.8 4.4 %attend.1 = (bf16[4,272,128]{2,1,0:T(8,128)(2,1)S(1)}, bf16[512,4096]{1,0:T(8,128)(2,1)S(1)}) custom-call(s32[128]{0:T(128)S(1)} %copy-done.1, bf16[4,64,512]{2,1,0:T(8,128)(2,1)S(1)} %all_to_all.15.q_ref, bf16[16,64,256]{2,1,0:T(8,128)(2,1)S(1)} %bitcast.4, bf16[16,64,256]{2,1,0:T(8,128)(2,1)S(1)} %collective-permute-done.1.other_ref, bf16[512,4096]{1,0:T(8,128)(2,1)} %ow_hbm.1), custom_call_target="tpu_custom_call" | custom-call | tf_op jit(solution)/shard_map/attend/pallas_call | solution.py:291
  79.2 13.3 %all_to_all.16.parts_ref = bf16[4,272,128]{2,1,0:T(8,128)(2,1)S(1)} all-to-all(bf16[4,272,128]{2,1,0:T(8,128)(2,1)S(1)} %get-tuple-element.17), channel_id=1, replica_groups=mesh['yh'=4,'z'=16,'row'=2,'x'=4,'yl'=2] {'yh'}, dimensions={0} | all-to-all | bytes 557056 | tf_op jit(solution)/shard_map/all_to_all | solution.py:304
  92.5 1.2 %output.1 = bf16[16,64,256]{2,1,0:T(8,128)(2,1)S(1)} custom-call(bf16[4,272,128]{2,1,0:T(8,128)(2,1)S(1)} %all_to_all.16.parts_ref, bf16[512,4096]{1,0:T(8,128)(2,1)S(1)} %get-tuple-element.18.ow_ref), custom_call_target="tpu_custom_call" | custom-call | tf_op jit(solution)/shard_map/output/pallas_call | solution.py:237
  93.6 15.8 %all_to_all.17.recv_ref = bf16[16,64,256]{2,1,0:T(8,128)(2,1)S(1)} all-to-all(bf16[16,64,256]{2,1,0:T(8,128)(2,1)S(1)} %output.1), channel_id=1, replica_groups=mesh['yh'=4,'z'=16,'row'=2,'x'=4,'yl'=2] {'row','x','yl'}, dimensions={0} | all-to-all | bytes 1048576 | tf_op jit(solution)/shard_map/all_to_all | solution.py:307
  109.4 0.7 gather.1
  (2 shorter events, 0.0 us)
Async XLA Ops:
  0.0 74.8 %copy-start.1 = (s32[128]{0:T(128)S(1)}, s32[128]{0:T(128)}, u32[]{:S(2)}) copy-start(s32[128]{0:T(128)} %order_ref.3) | copy-start | bytes 1540
  4.6 17.3 %collective-permute-start = (f32[64,768]{1,0:T(8,128)}, f32[64,768]{1,0:T(8,128)S(1)}, u32[]{:S(2)}, u32[]{:S(2)}) collective-permute-start(f32[64,768]{1,0:T(8,128)} %get-tuple-element.13), channel_id=1, source_target_pairs={{0,8},{8,0},{1,9},{9,1},{2,10},{10,2},{3,11},{11,3},{4,12},{12,4},... | collective-permute-start | bytes 589832 | tf_op jit(solution)/shard_map/ppermute | solution.py:270
  21.9 0.9 copy-start
  48.9 25.9 %collective-permute-start.1 = (bf16[16,64,256]{2,1,0:T(8,128)(2,1)S(1)}, bf16[16,64,256]{2,1,0:T(8,128)(2,1)S(1)}, u32[]{:S(2)}, u32[]{:S(2)}) collective-permute-start(bf16[16,64,256]{2,1,0:T(8,128)(2,1)S(1)} %bitcast.3), channel_id=1, source_target_pairs={{0,8},{8,0},{1,9},{9,1},{2,10},{10,2},{3,11},{11,3},{4,12},{12,4},... | collective-permute-start | bytes 1572872 | tf_op jit(solution)/shard_map/ppermute | solution.py:288

commit v2 on v1

--- a/solution.py
+++ b/solution.py
@@ -89,7 +89,7 @@
             pltpu.VMEM((rows, width), f32),
             pltpu.SemaphoreType.DMA((chunks, 4)),
         ],
-        compiler_params=params(60000),
+        compiler_params=params(16384),
         name="project",
     )(order, freqs, tokens, query_weight, key_weight, value_weight)
 
@@ -144,46 +144,49 @@
         ]
         return jnp.concatenate(pieces, axis=0)
 
-    k_low, v_low = both(0, part, 0), both(0, part, HD)
-    k_high, v_high = both(part, tok, 0), both(part, tok, HD)
+    ones = jnp.where(lax.broadcasted_iota(jnp.int32, (2 * keys, HD), 1) == 0, 1.0, 0.0).astype(bf16)
+    k_low, k_high = both(0, part, 0), both(part, tok, 0)
+    v_low = jnp.concatenate([both(0, part, HD), ones], axis=1)
+    v_high = jnp.concatenate([both(part, tok, HD), ones], axis=1)
     q_inner = lax.broadcasted_iota(jnp.int32, (rows, 1), 0) & (part - 1)
     spot = lax.broadcasted_iota(jnp.int32, (rows, HD), 1)
 
-    for a in range(peers_a):
+    for turn in range(peers_a):
+        a = (yh + turn) & (peers_a - 1)
         slot = 2 * (a * peers_e + z)
+        b_low, b_high = order_ref[slot], order_ref[slot + 1]
+        mine = q_ref.at[a]
 
         def stacked(first, last):
-            return jnp.concatenate(
-                [q_ref[a, first:last, h * HD : (h + 1) * HD] for h in range(heads)], axis=0
-            )
-
-        q_low, q_high = stacked(0, part), stacked(part, tok)
-        q_low_pos = order_ref[slot] * (2 * part) + row * part + q_inner
-        q_high_pos = order_ref[slot + 1] * (2 * part) + row * part + q_inner
-
-        s_ll = jnp.where(low_pos <= q_low_pos, dot_t(q_low, k_low), large_negative)
+            return [mine[first:last, h * HD : (h + 1) * HD] for h in range(heads)]
+
+        q_both = jnp.concatenate(stacked(0, part) + stacked(part, tok), axis=0)
+        s_low = dot_t(q_both, k_low)
+        s_ll, s_hl = s_low[:rows], s_low[rows:]
+        s_hh = dot_t(q_both[rows:], k_high)
+        if turn == 0:
+            s_ll = jnp.where(low_pos <= b_low * (2 * part) + row * part + q_inner, s_ll, large_negative)
+            s_hh = jnp.where(high_pos <= b_high * (2 * part) + row * part + q_inner, s_hh, large_negative)
+        else:
+            s_ll = s_ll + jnp.where(low_pos < b_low * (2 * part), 0.0, large_negative)
+            s_hh = s_hh + jnp.where(high_pos < b_high * (2 * part), 0.0, large_negative)
         m_low = jnp.maximum(jnp.max(s_ll, axis=1, keepdims=True), large_negative * 0.1)
-        p_ll = jnp.exp2((s_ll - m_low) * score_to_log2)
-        d_low = jnp.sum(p_ll, axis=1, keepdims=True)
-        o_low = jnp.dot(p_ll.astype(bf16), v_low, preferred_element_type=f32)
-
-        s_hl = dot_t(q_high, k_low)
-        s_hh = jnp.where(high_pos <= q_high_pos, dot_t(q_high, k_high), large_negative)
         m_high = jnp.maximum(
             jnp.max(s_hl, axis=1, keepdims=True), jnp.max(s_hh, axis=1, keepdims=True)
         )
-        p_hl = jnp.exp2((s_hl - m_high) * score_to_log2)
-        p_hh = jnp.exp2((s_hh - m_high) * score_to_log2)
-        d_high = jnp.sum(p_hl, axis=1, keepdims=True) + jnp.sum(p_hh, axis=1, keepdims=True)
-        o_high = jnp.dot(p_hl.astype(bf16), v_low, preferred_element_type=f32) + jnp.dot(
-            p_hh.astype(bf16), v_high, preferred_element_type=f32
-        )
+        p_ll = jnp.exp2((s_ll - m_low) * score_to_log2).astype(bf16)
+        p_hl = jnp.exp2((s_hl - m_high) * score_to_log2).astype(bf16)
+        p_hh = jnp.exp2((s_hh - m_high) * score_to_log2).astype(bf16)
+        o_both = jnp.dot(jnp.concatenate([p_ll, p_hl], axis=0), v_low, preferred_element_type=f32)
+        o_low = o_both[:rows]
+        o_high = o_both[rows:] + jnp.dot(p_hh, v_high, preferred_element_type=f32)
 
         logs = jnp.zeros((rows, HD), f32)
-        for i, (m, d, o) in enumerate(((m_low, d_low, o_low), (m_high, d_high, o_high))):
+        for i, (m, o) in enumerate(((m_low, o_low), (m_high, o_high))):
+            d = o[:, HD : HD + 1]
             seen = d > 0.0
             safe = jnp.where(seen, d, 1.0)
-            out_ref[a, i * rows : (i + 1) * rows, :] = (o / safe).astype(bf16)
+            out_ref[a, i * rows : (i + 1) * rows, :] = (o[:, :HD] * (1.0 / safe)).astype(bf16)
             log = jnp.where(seen, m * score_to_log2 + jnp.log2(safe), large_negative)
             for j in range(3):
                 piece = log.astype(bf16).astype(f32)
@@ -191,6 +194,22 @@
                 log = log - piece
         out_ref[a, 2 * rows :, :] = logs.T[:16, :].astype(bf16)
     fetch.wait()
+
+
+def attend(block_order, queries, own_keys, other_keys, output_weight):
+    peers, tok, width = queries.shape
+    return pl.pallas_call(
+        attend_kernel,
+        in_specs=[SMEM, VMEM, VMEM, VMEM, HBM],
+        out_specs=[VMEM] * 2,
+        out_shape=[
+            jax.ShapeDtypeStruct((peers, tok * width // HD + 16, HD), bf16),
+            jax.ShapeDtypeStruct(output_weight.shape, bf16),
+        ],
+        scratch_shapes=[pltpu.SemaphoreType.DMA],
+        compiler_params=params(24576),
+        name="attend",
+    )(block_order, queries, own_keys, other_keys, output_weight)
 
 
 def output_kernel(parts_ref, ow_ref, out_ref, att):
@@ -260,12 +279,15 @@
 def body(tokens, block_order, query_weight, key_weight, value_weight, output_weight):
     rows_here = tokens.shape[0]
     tok = rows_here // 2
-    part = tok // 2
     q_width = query_weight.shape[1]
 
     half_width = HD // 2
     freqs = rope_theta ** (-(jnp.arange(half_width, dtype=f32) * 2.0 / HD))
     freqs = jnp.concatenate([freqs, freqs])[None]
+    block_order, tokens, query_weight, key_weight, value_weight, output_weight = (
+        pltpu.with_memory_space_constraint(array, pltpu.HBM)
+        for array in (block_order, tokens, query_weight, key_weight, value_weight, output_weight)
+    )
     own, send, angles = project(block_order, freqs, tokens, query_weight, key_weight, value_weight)
     recv = lax.ppermute(send, "row", [(0, 1), (1, 0)])
 
@@ -287,20 +309,7 @@
     own_keys = lax.all_gather(key_values, "z")
     other_keys = lax.ppermute(own_keys, "row", [(0, 1), (1, 0)])
 
-    heads = q_width // HD
-    result, fetched = pl.pallas_call(
-        attend_kernel,
-        in_specs=[SMEM, VMEM, VMEM, VMEM, HBM],
-        out_specs=[VMEM] * 2,
-        out_shape=[
-            jax.ShapeDtypeStruct((peers_a, 2 * heads * part + 16, HD), bf16),
-            jax.ShapeDtypeStruct(output_weight.shape, bf16),
-        ],
-        scratch_shapes=[pltpu.SemaphoreType.DMA],
-        compiler_params=params(48000),
-        name="attend",
-    )(block_order, all_queries, own_keys, other_keys, output_weight)
-
+    result, fetched = attend(block_order, all_queries, own_keys, other_keys, output_weight)
     parts = lax.all_to_all(result, "yh", 0, 0)
     across = ("row", "x", "yl")
     partial_out = output(parts, fetched, tok, lax.axis_size(across))

time: 111 us -> 107 us (0.964)
  Pallas kernels: 10.3 us -> 8.59 us
  local copies, waits for them, and re-layouts: 1.84 us -> 0.15 us
  transfers between devices with their start and end apart: 2 -> 2, of which waited for: 1 -> 1; matrix products, arithmetic and copies ran while one was open for 1% -> 0% of each run, Pallas kernels for 0% -> 0%
where the time goes in v2:
time: 107 us
  blocking collectives  71.5 us (67%)
  starting transfers between devices  25.3 us (24%)
  Pallas kernels  8.59 us (8%)
    all_gather x1, blocking collectives, body(): own_keys = lax.all_gather(key_values, 'z')  25.9 us
    all_to_all x1, blocking collectives, body(): all_queries = lax.all_to_all(spread, 'yh', 0, 0)  16.5 us
    ppermute x1, starting transfers between devices, body(): recv = lax.ppermute(send, 'row', [(0, 1), (1, 0)])  16 us
    all_to_all x1, blocking collectives, body(): shares = lax.all_to_all(partial_out, across, 0, 0)  15.8 us
    all_to_all x1, blocking collectives, body(): parts = lax.all_to_all(result, 'yh', 0, 0)  13.2 us
    ppermute x1, starting transfers between devices, body(): other_keys = lax.ppermute(own_keys, 'row', [(0, 1), (1, 0)])  9.32 us
    pallas_call x1, Pallas kernels, attend(): pl.pallas_call(attend_kernel, in_specs=[SMEM, VMEM, VMEM, VMEM, HBM], out...  3.45 us
    pallas_call x1, Pallas kernels, project(): pl.pallas_call(partial(project_kernel, lax.axis_size('z')), in_specs=[SME...  3.17 us
  transfers between devices with their start and end apart: 2, of which 1 were waited for; matrix products, arithmetic and copies ran while one was open for 0% of the time, Pallas kernels for 0%

profile of v2, /device:TPU:1, one launch (start us, length us, event | category | flops | bytes accessed | tf_op | source)
XLA Modules:
  0.0 106.7 jit_solution(4826368071973664296)
XLA Ops:
  0.0 0.1 maximum_bitcast_fusion.freq_ref
  0.1 3.2 %project.1 = (f32[64,768]{1,0:T(8,128)S(1)}, f32[64,768]{1,0:T(8,128)S(1)}, f32[64,128]{1,0:T(8,128)S(1)}) custom-call(s32[128]{0:T(128)} %order_ref.3, f32[1,128]{1,0:T(1,128)S(1)} %maximum_bitcast_fusion.freq_ref, bf16[128,2048]{1,0:T(8,128)(2,1)} %tok_ref.1, bf16[2048,512]{1,0:T(8,128)(2,1)} %qw_ref.1, bf16[2048,128]{1,0:T(8,128)(2,1)} %kw_ref.1, ...), custom_call_target="tpu_custom_call" | custom-call | tf_op jit(solution)/shard_map/project/pallas_call | solution.py:81
  3.3 16.0 %collective-permute-start = (f32[64,768]{1,0:T(8,128)S(1)}, f32[64,768]{1,0:T(8,128)S(1)}, u32[]{:S(2)}, u32[]{:S(2)}) collective-permute-start(f32[64,768]{1,0:T(8,128)S(1)} %get-tuple-element.13), channel_id=1, source_target_pairs={{0,8},{8,0},{1,9},{9,1},{2,10},{10,2},{3,11},{11,3},{4,12},{12,4},... | collective-permute-start | bytes 589832 | tf_op jit(solution)/shard_map/ppermute | solution.py:292
  19.3 0.1 fusion
  19.4 0.9 collective-permute-done.recv_ref
  20.3 0.1 rope.1
  20.5 25.9 %all-gather = bf16[1024,256]{1,0:T(8,128)(2,1)S(1)} all-gather(bf16[64,256]{1,0:T(8,128)(2,1)S(1)} %get-tuple-element.16), channel_id=2, replica_groups=mesh['yh'=4,'z'=16,'row'=2,'x'=4,'yl'=2] {'z'}, dimensions={0}, use_global_device_ids=true | all-gather | bytes 557056 | tf_op jit(solution)/shard_map/all_gather | solution.py:309
  46.4 9.3 %collective-permute-start.1 = (bf16[16,64,256]{2,1,0:T(8,128)(2,1)S(1)}, bf16[16,64,256]{2,1,0:T(8,128)(2,1)S(1)}, u32[]{:S(2)}, u32[]{:S(2)}) collective-permute-start(bf16[16,64,256]{2,1,0:T(8,128)(2,1)S(1)} %bitcast.3), channel_id=1, source_target_pairs={{0,8},{8,0},{1,9},{9,1},{2,10},{10,2},{3,11},{11,3},{4,12},{12,4},... | collective-permute-start | bytes 1572872 | tf_op jit(solution)/shard_map/ppermute | solution.py:310
  55.7 16.5 %all_to_all.15.q_ref = bf16[4,64,512]{2,1,0:T(8,128)(2,1)S(1)} all-to-all(bf16[4,64,512]{2,1,0:T(8,128)(2,1)S(1)} %broadcast_in_dim.10), channel_id=1, replica_groups=mesh['yh'=4,'z'=16,'row'=2,'x'=4,'yl'=2] {'yh'}, dimensions={0} | all-to-all | bytes 524288 | tf_op jit(solution)/shard_map/all_to_all | solution.py:308
  72.3 0.0 collective-permute-done.1.other_ref
  72.3 3.5 %attend.1 = (bf16[4,272,128]{2,1,0:T(8,128)(2,1)S(1)}, bf16[512,4096]{1,0:T(8,128)(2,1)S(1)}) custom-call(s32[128]{0:T(128)} %order_ref.3, bf16[4,64,512]{2,1,0:T(8,128)(2,1)S(1)} %all_to_all.15.q_ref, bf16[16,64,256]{2,1,0:T(8,128)(2,1)S(1)} %bitcast.4, bf16[16,64,256]{2,1,0:T(8,128)(2,1)S(1)} %collective-permute-done.1.other_ref, bf16[512,4096]{1,0:T(8,128)(2,1)} %ow_hbm.1), custom_call_target="tpu_custom_call" | custom-call | tf_op jit(solution)/shard_map/attend/pallas_call | solution.py:201
  75.7 13.2 %all_to_all.16.parts_ref = bf16[4,272,128]{2,1,0:T(8,128)(2,1)S(1)} all-to-all(bf16[4,272,128]{2,1,0:T(8,128)(2,1)S(1)} %get-tuple-element.17), channel_id=1, replica_groups=mesh['yh'=4,'z'=16,'row'=2,'x'=4,'yl'=2] {'yh'}, dimensions={0} | all-to-all | bytes 557056 | tf_op jit(solution)/shard_map/all_to_all | solution.py:313
  89.0 1.1 %output.1 = bf16[16,64,256]{2,1,0:T(8,128)(2,1)S(1)} custom-call(bf16[4,272,128]{2,1,0:T(8,128)(2,1)S(1)} %all_to_all.16.parts_ref, bf16[512,4096]{1,0:T(8,128)(2,1)S(1)} %get-tuple-element.18.ow_ref), custom_call_target="tpu_custom_call" | custom-call | tf_op jit(solution)/shard_map/output/pallas_call | solution.py:256
  90.1 15.8 %all_to_all.17.recv_ref = bf16[16,64,256]{2,1,0:T(8,128)(2,1)S(1)} all-to-all(bf16[16,64,256]{2,1,0:T(8,128)(2,1)S(1)} %output.1), channel_id=1, replica_groups=mesh['yh'=4,'z'=16,'row'=2,'x'=4,'yl'=2] {'row','x','yl'}, dimensions={0} | all-to-all | bytes 1048576 | tf_op jit(solution)/shard_map/all_to_all | solution.py:316
  106.0 0.7 gather.1
  (2 shorter events, 0.0 us)
Async XLA Ops:
  3.3 17.1 %collective-permute-start = (f32[64,768]{1,0:T(8,128)S(1)}, f32[64,768]{1,0:T(8,128)S(1)}, u32[]{:S(2)}, u32[]{:S(2)}) collective-permute-start(f32[64,768]{1,0:T(8,128)S(1)} %get-tuple-element.13), channel_id=1, source_target_pairs={{0,8},{8,0},{1,9},{9,1},{2,10},{10,2},{3,11},{11,3},{4,12},{12,4},... | collective-permute-start | bytes 589832 | tf_op jit(solution)/shard_map/ppermute | solution.py:292
  46.4 25.9 %collective-permute-start.1 = (bf16[16,64,256]{2,1,0:T(8,128)(2,1)S(1)}, bf16[16,64,256]{2,1,0:T(8,128)(2,1)S(1)}, u32[]{:S(2)}, u32[]{:S(2)}) collective-permute-start(bf16[16,64,256]{2,1,0:T(8,128)(2,1)S(1)} %bitcast.3), channel_id=1, source_target_pairs={{0,8},{8,0},{1,9},{9,1},{2,10},{10,2},{3,11},{11,3},{4,12},{12,4},... | collective-permute-start | bytes 1572872 | tf_op jit(solution)/shard_map/ppermute | solution.py:310

commit v3 on v2

--- a/solution.py
+++ b/solution.py
@@ -106,9 +106,12 @@
         if h < heads:
             q_ref[:, cols] = y
         else:
-            kv_ref[:, :HD] = y
+            for e in range(kv_ref.shape[0]):
+                kv_ref[e, :, :HD] = y
     cols = slice((heads + 1) * HD, (heads + 2) * HD)
-    kv_ref[:, HD:] = (own_ref[:, cols] + recv_ref[:, cols]).astype(bf16)
+    y = (own_ref[:, cols] + recv_ref[:, cols]).astype(bf16)
+    for e in range(kv_ref.shape[0]):
+        kv_ref[e, :, HD:] = y
 
 
 def attend_kernel(order_ref, q_ref, own_ref, other_ref, ow_hbm, out_ref, ow_ref, sem):
@@ -297,16 +300,14 @@
         out_specs=[VMEM] * 2,
         out_shape=[
             jax.ShapeDtypeStruct((tok, q_width), bf16),
-            jax.ShapeDtypeStruct((tok, 2 * HD), bf16),
+            jax.ShapeDtypeStruct((lax.axis_size("z"), tok, 2 * HD), bf16),
         ],
         compiler_params=params(8192),
         name="rope",
     )(own, recv, jnp.cos(angles), jnp.sin(angles))
 
-    peers_a = lax.axis_size("yh")
-    spread = jnp.broadcast_to(queries[None], (peers_a, tok, q_width))
-    all_queries = lax.all_to_all(spread, "yh", 0, 0)
-    own_keys = lax.all_gather(key_values, "z")
+    own_keys = lax.all_to_all(key_values, "z", 0, 0)
+    all_queries = lax.all_gather(queries, "yh")
     other_keys = lax.ppermute(own_keys, "row", [(0, 1), (1, 0)])
 
     result, fetched = attend(block_order, all_queries, own_keys, other_keys, output_weight)

time: 107 us -> 109 us (1.019)
  blocking collectives: 71.5 us -> 73.5 us
    all_to_all x1, blocking collectives: 16.5 us -> 28.5 us  [body(): own_keys = lax.all_to_all(key_values, 'z', 0, 0)]
    all_gather x1, blocking collectives: 25.9 us -> 14.4 us  [body(): all_queries = lax.all_gather(queries, 'yh')]
    all_to_all x1, blocking collectives: 15.8 us -> 18 us  [body(): shares = lax.all_to_all(partial_out, across, 0, 0)]
where the time goes in v3:
time: 109 us; the launch traced here: 108 us
  blocking collectives  73.5 us (67%)
  starting transfers between devices  25 us (23%)
  Pallas kernels  8.62 us (8%)
    all_to_all x1, blocking collectives, body(): own_keys = lax.all_to_all(key_values, 'z', 0, 0)  28.5 us
    all_to_all x1, blocking collectives, body(): shares = lax.all_to_all(partial_out, across, 0, 0)  18 us
    ppermute x1, starting transfers between devices, body(): recv = lax.ppermute(send, 'row', [(0, 1), (1, 0)])  16 us
    all_gather x1, blocking collectives, body(): all_queries = lax.all_gather(queries, 'yh')  14.4 us
    all_to_all x1, blocking collectives, body(): parts = lax.all_to_all(result, 'yh', 0, 0)  12.5 us
    ppermute x1, starting transfers between devices, body(): other_keys = lax.ppermute(own_keys, 'row', [(0, 1), (1, 0)])  9.03 us
    pallas_call x1, Pallas kernels, attend(): pl.pallas_call(attend_kernel, in_specs=[SMEM, VMEM, VMEM, VMEM, HBM], out...  3.45 us
    pallas_call x1, Pallas kernels, project(): pl.pallas_call(partial(project_kernel, lax.axis_size('z')), in_specs=[SME...  3.17 us
  transfers between devices with their start and end apart: 2, of which 1 were waited for; matrix products, arithmetic and copies ran while one was open for 0% of the time, Pallas kernels for 0%

profile of v3, /device:TPU:1, one launch (start us, length us, event | category | flops | bytes accessed | tf_op | source)
XLA Modules:
  0.0 108.3 jit_solution(5492457473529918032)
XLA Ops:
  0.0 0.1 maximum_bitcast_fusion.freq_ref
  0.1 3.2 %project.1 = (f32[64,768]{1,0:T(8,128)S(1)}, f32[64,768]{1,0:T(8,128)S(1)}, f32[64,128]{1,0:T(8,128)S(1)}) custom-call(s32[128]{0:T(128)} %order_ref.3, f32[1,128]{1,0:T(1,128)S(1)} %maximum_bitcast_fusion.freq_ref, bf16[128,2048]{1,0:T(8,128)(2,1)} %tok_ref.1, bf16[2048,512]{1,0:T(8,128)(2,1)} %qw_ref.1, bf16[2048,128]{1,0:T(8,128)(2,1)} %kw_ref.1, ...), custom_call_target="tpu_custom_call" | custom-call | tf_op jit(solution)/shard_map/project/pallas_call | solution.py:81
  3.3 16.0 %collective-permute-start = (f32[64,768]{1,0:T(8,128)S(1)}, f32[64,768]{1,0:T(8,128)S(1)}, u32[]{:S(2)}, u32[]{:S(2)}) collective-permute-start(f32[64,768]{1,0:T(8,128)S(1)} %get-tuple-element.13), channel_id=1, source_target_pairs={{0,8},{8,0},{1,9},{9,1},{2,10},{10,2},{3,11},{11,3},{4,12},{12,4},... | collective-permute-start | bytes 589832 | tf_op jit(solution)/shard_map/ppermute | solution.py:295
  19.3 0.1 fusion
  19.4 0.9 collective-permute-done.recv_ref
  20.3 0.2 rope.1
  20.5 28.5 %all_to_all.15.own_ref = bf16[16,64,256]{2,1,0:T(8,128)(2,1)S(1)} all-to-all(bf16[16,64,256]{2,1,0:T(8,128)(2,1)S(1)} %get-tuple-element.16), channel_id=1, replica_groups=mesh['yh'=4,'z'=16,'row'=2,'x'=4,'yl'=2] {'z'}, dimensions={0} | all-to-all | bytes 1048576 | tf_op jit(solution)/shard_map/all_to_all | solution.py:309
  49.0 9.0 %collective-permute-start.1 = (bf16[16,64,256]{2,1,0:T(8,128)(2,1)S(1)}, bf16[16,64,256]{2,1,0:T(8,128)(2,1)S(1)}, u32[]{:S(2)}, u32[]{:S(2)}) collective-permute-start(bf16[16,64,256]{2,1,0:T(8,128)(2,1)S(1)} %all_to_all.15.own_ref), channel_id=1, source_target_pairs={{0,8},{8,0},{1,9},{9,1},{2,10},{10,2},{3,11},{11,3},{4,12},{12,4},... | collective-permute-start | bytes 1572872 | tf_op jit(solution)/shard_map/ppermute | solution.py:311
  58.0 14.4 %all-gather = bf16[256,512]{1,0:T(8,128)(2,1)S(1)} all-gather(bf16[64,512]{1,0:T(8,128)(2,1)S(1)} %get-tuple-element.15), channel_id=2, replica_groups=mesh['yh'=4,'z'=16,'row'=2,'x'=4,'yl'=2] {'yh'}, dimensions={0}, use_global_device_ids=true | all-gather | bytes 327680 | tf_op jit(solution)/shard_map/all_gather | solution.py:310
  72.5 0.0 collective-permute-done.1.other_ref
  72.5 3.4 %attend.1 = (bf16[4,272,128]{2,1,0:T(8,128)(2,1)S(1)}, bf16[512,4096]{1,0:T(8,128)(2,1)S(1)}) custom-call(s32[128]{0:T(128)} %order_ref.3, bf16[4,64,512]{2,1,0:T(8,128)(2,1)S(1)} %bitcast.3, bf16[16,64,256]{2,1,0:T(8,128)(2,1)S(1)} %all_to_all.15.own_ref, bf16[16,64,256]{2,1,0:T(8,128)(2,1)S(1)} %collective-permute-done.1.other_ref, bf16[512,4096]{1,0:T(8,128)(2,1)} %ow_hbm.1), custom_call_target="tpu_custom_call" | custom-call | tf_op jit(solution)/shard_map/attend/pallas_call | solution.py:204
  75.9 12.5 %all_to_all.16.parts_ref = bf16[4,272,128]{2,1,0:T(8,128)(2,1)S(1)} all-to-all(bf16[4,272,128]{2,1,0:T(8,128)(2,1)S(1)} %get-tuple-element.17), channel_id=1, replica_groups=mesh['yh'=4,'z'=16,'row'=2,'x'=4,'yl'=2] {'yh'}, dimensions={0} | all-to-all | bytes 557056 | tf_op jit(solution)/shard_map/all_to_all | solution.py:314
  88.4 1.1 %output.1 = bf16[16,64,256]{2,1,0:T(8,128)(2,1)S(1)} custom-call(bf16[4,272,128]{2,1,0:T(8,128)(2,1)S(1)} %all_to_all.16.parts_ref, bf16[512,4096]{1,0:T(8,128)(2,1)S(1)} %get-tuple-element.18.ow_ref), custom_call_target="tpu_custom_call" | custom-call | tf_op jit(solution)/shard_map/output/pallas_call | solution.py:259
  89.6 18.0 %all_to_all.17.recv_ref = bf16[16,64,256]{2,1,0:T(8,128)(2,1)S(1)} all-to-all(bf16[16,64,256]{2,1,0:T(8,128)(2,1)S(1)} %output.1), channel_id=1, replica_groups=mesh['yh'=4,'z'=16,'row'=2,'x'=4,'yl'=2] {'row','x','yl'}, dimensions={0} | all-to-all | bytes 1048576 | tf_op jit(solution)/shard_map/all_to_all | solution.py:317
  107.6 0.7 gather.1
  (1 shorter events, 0.0 us)
Async XLA Ops:
  3.3 17.1 %collective-permute-start = (f32[64,768]{1,0:T(8,128)S(1)}, f32[64,768]{1,0:T(8,128)S(1)}, u32[]{:S(2)}, u32[]{:S(2)}) collective-permute-start(f32[64,768]{1,0:T(8,128)S(1)} %get-tuple-element.13), channel_id=1, source_target_pairs={{0,8},{8,0},{1,9},{9,1},{2,10},{10,2},{3,11},{11,3},{4,12},{12,4},... | collective-permute-start | bytes 589832 | tf_op jit(solution)/shard_map/ppermute | solution.py:295
  49.0 23.5 %collective-permute-start.1 = (bf16[16,64,256]{2,1,0:T(8,128)(2,1)S(1)}, bf16[16,64,256]{2,1,0:T(8,128)(2,1)S(1)}, u32[]{:S(2)}, u32[]{:S(2)}) collective-permute-start(bf16[16,64,256]{2,1,0:T(8,128)(2,1)S(1)} %all_to_all.15.own_ref), channel_id=1, source_target_pairs={{0,8},{8,0},{1,9},{9,1},{2,10},{10,2},{3,11},{11,3},{4,12},{12,4},... | collective-permute-start | bytes 1572872 | tf_op jit(solution)/shard_map/ppermute | solution.py:311

commit v4 on v3

--- a/solution.py
+++ b/solution.py
@@ -30,22 +30,20 @@
     return lax.axis_index("yh"), lax.axis_index("z"), lax.axis_index("row")
 
 
-def project_kernel(
-    peers, order_ref, freq_ref, tok_ref, qw_ref, kw_ref, vw_ref, own_ref, send_ref, angle_ref, tok, weight, acc, sems
-):
-    q_width = qw_ref.shape[1]
+def project_kernel(peers, count, order_ref, freq_ref, tok_ref, *refs):
+    weight_refs = refs[:count]
+    own_ref, send_ref, angle_ref, tok, weight, acc, sems = refs[count:]
     depth = tok_ref.shape[1]
     chunks = sems.shape[0]
     blk = depth // chunks
     copies = []
     for c in range(chunks):
         at = slice(c * blk, (c + 1) * blk)
-        pairs = (
-            (tok_ref.at[:, at], tok.at[:, at]),
-            (qw_ref.at[at], weight.at[at, :q_width]),
-            (kw_ref.at[at], weight.at[at, q_width : q_width + HD]),
-            (vw_ref.at[at], weight.at[at, q_width + HD :]),
-        )
+        pairs = [(tok_ref.at[:, at], tok.at[:, at])]
+        first = 0
+        for ref in weight_refs:
+            pairs.append((ref.at[at], weight.at[at, first : first + ref.shape[1]]))
+            first += ref.shape[1]
         copies.append([pltpu.make_async_copy(*pair, sems.at[c, k]) for k, pair in enumerate(pairs)])
         for copy in copies[-1]:
             copy.start()
@@ -73,45 +71,50 @@
         send_ref[k * part : (k + 1) * part, :] = acc[theirs, :]
 
 
-def project(order, freqs, tokens, query_weight, key_weight, value_weight):
+def project(order, freqs, tokens, *weights):
     rows, depth = tokens.shape
-    width = query_weight.shape[1] + 2 * HD
+    width = sum(weight.shape[1] for weight in weights)
     chunks = 4
     out = jax.ShapeDtypeStruct((rows // 2, width), f32)
     return pl.pallas_call(
-        partial(project_kernel, lax.axis_size("z")),
-        in_specs=[SMEM, VMEM] + [HBM] * 4,
+        partial(project_kernel, lax.axis_size("z"), len(weights)),
+        in_specs=[SMEM, VMEM, HBM] + [HBM] * len(weights),
         out_specs=[VMEM] * 3,
         out_shape=[out, out, jax.ShapeDtypeStruct((rows // 2, HD), f32)],
         scratch_shapes=[
             pltpu.VMEM((rows, depth), bf16),
             pltpu.VMEM((depth, width), bf16),
             pltpu.VMEM((rows, width), f32),
-            pltpu.SemaphoreType.DMA((chunks, 4)),
+            pltpu.SemaphoreType.DMA((chunks, 1 + len(weights))),
         ],
         compiler_params=params(16384),
         name="project",
-    )(order, freqs, tokens, query_weight, key_weight, value_weight)
-
-
-def rope_kernel(own_ref, recv_ref, cos_ref, sin_ref, q_ref, kv_ref):
+    )(order, freqs, tokens, *weights)
+
+
+def rope_kernel(turned, own_ref, recv_ref, cos_ref, sin_ref, out_ref):
     cosine = cos_ref[...]
     lane = lax.broadcasted_iota(jnp.int32, sin_ref.shape, 1)
     sine = jnp.where(lane < HD // 2, -sin_ref[...], sin_ref[...])
-    heads = q_ref.shape[1] // HD
-    for h in range(heads + 1):
+    for h in range(out_ref.shape[2] // HD):
         cols = slice(h * HD, (h + 1) * HD)
         x = own_ref[:, cols] + recv_ref[:, cols]
-        y = (x * cosine + pltpu.roll(x, HD // 2, 1) * sine).astype(bf16)
-        if h < heads:
-            q_ref[:, cols] = y
-        else:
-            for e in range(kv_ref.shape[0]):
-                kv_ref[e, :, :HD] = y
-    cols = slice((heads + 1) * HD, (heads + 2) * HD)
-    y = (own_ref[:, cols] + recv_ref[:, cols]).astype(bf16)
-    for e in range(kv_ref.shape[0]):
-        kv_ref[e, :, HD:] = y
+        if h < turned:
+            x = x * cosine + pltpu.roll(x, HD // 2, 1) * sine
+        for e in range(out_ref.shape[0]):
+            out_ref[e, :, cols] = x.astype(bf16)
+
+
+def rope(own, send, cosine, sine, turned, copies):
+    recv = lax.ppermute(send, "row", [(0, 1), (1, 0)])
+    return pl.pallas_call(
+        partial(rope_kernel, turned),
+        in_specs=[VMEM] * 4,
+        out_specs=VMEM,
+        out_shape=jax.ShapeDtypeStruct((copies, *own.shape), bf16),
+        compiler_params=params(8192),
+        name="rope",
+    )(own, recv, cosine, sine)
 
 
 def attend_kernel(order_ref, q_ref, own_ref, other_ref, ow_hbm, out_ref, ow_ref, sem):
@@ -291,22 +294,12 @@
         pltpu.with_memory_space_constraint(array, pltpu.HBM)
         for array in (block_order, tokens, query_weight, key_weight, value_weight, output_weight)
     )
-    own, send, angles = project(block_order, freqs, tokens, query_weight, key_weight, value_weight)
-    recv = lax.ppermute(send, "row", [(0, 1), (1, 0)])
-
-    queries, key_values = pl.pallas_call(
-        rope_kernel,
-        in_specs=[VMEM] * 4,
-        out_specs=[VMEM] * 2,
-        out_shape=[
-            jax.ShapeDtypeStruct((tok, q_width), bf16),
-            jax.ShapeDtypeStruct((lax.axis_size("z"), tok, 2 * HD), bf16),
-        ],
-        compiler_params=params(8192),
-        name="rope",
-    )(own, recv, jnp.cos(angles), jnp.sin(angles))
-
+    own, send, angles = project(block_order, freqs, tokens, key_weight, value_weight)
+    cosine, sine = jnp.cos(angles), jnp.sin(angles)
+    key_values = rope(own, send, cosine, sine, 1, lax.axis_size("z"))
     own_keys = lax.all_to_all(key_values, "z", 0, 0)
+    own, send, _ = project(block_order, freqs, tokens, query_weight)
+    queries = rope(own, send, cosine, sine, q_width // HD, 1)[0]
     all_queries = lax.all_gather(queries, "yh")
     other_keys = lax.ppermute(own_keys, "row", [(0, 1), (1, 0)])
 

time: 109 us -> 115 us (1.055)
  Pallas kernels: 8.62 us -> 11.2 us
  starting transfers between devices: 25 us -> 26.9 us
    pallas_call x2 -> x4, Pallas kernels: 3.32 us -> 5.84 us  [the longest x2 5.62 us: project(): pl.pallas_call(partial(project_kernel, lax.axis_size('z'), len(weights)),...]
    ppermute x1 -> x2, starting transfers between devices: 16 us -> 17.9 us  [rope(): recv = lax.ppermute(send, 'row', [(0, 1), (1, 0)])]
  transfers between devices with their start and end apart: 2 -> 3, of which waited for: 1 -> 2; matrix products, arithmetic and copies ran while one was open for 0% -> 0% of each run, Pallas kernels for 0% -> 3%
where the time goes in v4:
time: 115 us; the launch traced here: 114 us
  blocking collectives  74 us (64%)
  starting transfers between devices  26.9 us (23%)
  Pallas kernels  11.2 us (10%)
  waiting for transfers between devices  2.06 us (2%)
    all_to_all x1, blocking collectives, body(): own_keys = lax.all_to_all(key_values, 'z', 0, 0)  28.5 us
    all_to_all x1, blocking collectives, body(): shares = lax.all_to_all(partial_out, across, 0, 0)  18.4 us
    ppermute x2, starting transfers between devices, rope(): recv = lax.ppermute(send, 'row', [(0, 1), (1, 0)])  17.9 us
    all_gather x1, blocking collectives, body(): all_queries = lax.all_gather(queries, 'yh')  14.1 us
    all_to_all x1, blocking collectives, body(): parts = lax.all_to_all(result, 'yh', 0, 0)  12.9 us
    ppermute x1, starting transfers between devices, body(): other_keys = lax.ppermute(own_keys, 'row', [(0, 1), (1, 0)])  9 us
    pallas_call x2, Pallas kernels, project(): pl.pallas_call(partial(project_kernel, lax.axis_size('z'), len(weights)),...  5.62 us
    pallas_call x1, Pallas kernels, attend(): pl.pallas_call(attend_kernel, in_specs=[SMEM, VMEM, VMEM, VMEM, HBM], out...  3.46 us
  transfers between devices with their start and end apart: 3, of which 2 were waited for; matrix products, arithmetic and copies ran while one was open for 0% of the time, Pallas kernels for 3%

profile of v4, /device:TPU:1, one launch (start us, length us, event | category | flops | bytes accessed | tf_op | source)
XLA Modules:
  0.0 114.4 jit_solution(2363625357931306167)
XLA Ops:
  0.0 0.1 maximum_bitcast_fusion.freq_ref
  0.1 2.5 %project.3 = (f32[64,256]{1,0:T(8,128)S(1)}, f32[64,256]{1,0:T(8,128)S(1)}, f32[64,128]{1,0:T(8,128)S(1)}) custom-call(s32[128]{0:T(128)} %order_ref.5, f32[1,128]{1,0:T(1,128)S(1)} %maximum_bitcast_fusion.freq_ref, bf16[128,2048]{1,0:T(8,128)(2,1)} %tok_ref.3, bf16[2048,128]{1,0:T(8,128)(2,1)} %refs_0_.3, bf16[2048,128]{1,0:T(8,128)(2,1)} %refs_1_.1), custom_call_target="tpu_custom_call" | custom-call | tf_op jit(solution)/shard_map/project/pallas_call | solution.py:79
  2.6 16.0 %collective-permute-start.1 = (f32[64,256]{1,0:T(8,128)S(1)}, f32[64,256]{1,0:T(8,128)S(1)}, u32[]{:S(2)}, u32[]{:S(2)}) collective-permute-start(f32[64,256]{1,0:T(8,128)S(1)} %get-tuple-element.16), channel_id=1, source_target_pairs={{0,8},{8,0},{1,9},{9,1},{2,10},{10,2},{3,11},{11,3},{4,12},{12,4},... | collective-permute-start | bytes 196616 | tf_op jit(solution)/shard_map/ppermute | solution.py:109
  18.7 0.1 fusion
  18.8 0.7 collective-permute-done.1.recv_ref
  19.6 0.1 rope.3
  19.7 28.5 %all_to_all.15.own_ref = bf16[16,64,256]{2,1,0:T(8,128)(2,1)S(1)} all-to-all(bf16[16,64,256]{2,1,0:T(8,128)(2,1)S(1)} %rope.3), channel_id=1, replica_groups=mesh['yh'=4,'z'=16,'row'=2,'x'=4,'yl'=2] {'z'}, dimensions={0} | all-to-all | bytes 1048576 | tf_op jit(solution)/shard_map/all_to_all | solution.py:300
  48.2 9.0 %collective-permute-start.2 = (bf16[16,64,256]{2,1,0:T(8,128)(2,1)S(1)}, bf16[16,64,256]{2,1,0:T(8,128)(2,1)S(1)}, u32[]{:S(2)}, u32[]{:S(2)}) collective-permute-start(bf16[16,64,256]{2,1,0:T(8,128)(2,1)S(1)} %all_to_all.15.own_ref), channel_id=1, source_target_pairs={{0,8},{8,0},{1,9},{9,1},{2,10},{10,2},{3,11},{11,3},{4,12},{12,4},... | collective-permute-start | bytes 1572872 | tf_op jit(solution)/shard_map/ppermute | solution.py:304
  57.2 3.1 %project.2 = (f32[64,512]{1,0:T(8,128)S(1)}, f32[64,512]{1,0:T(8,128)S(1)}, f32[64,128]{1,0:T(8,128)}) custom-call(s32[128]{0:T(128)} %order_ref.5, f32[1,128]{1,0:T(1,128)S(1)} %maximum_bitcast_fusion.freq_ref, bf16[128,2048]{1,0:T(8,128)(2,1)} %tok_ref.3, bf16[2048,512]{1,0:T(8,128)(2,1)} %refs_0_.2), custom_call_target="tpu_custom_call" | custom-call | tf_op jit(solution)/shard_map/project/pallas_call | solution.py:79
  60.3 1.9 %collective-permute-start = (f32[64,512]{1,0:T(8,128)S(1)}, f32[64,512]{1,0:T(8,128)S(1)}, u32[]{:S(2)}, u32[]{:S(2)}) collective-permute-start(f32[64,512]{1,0:T(8,128)S(1)} %get-tuple-element.13), channel_id=1, source_target_pairs={{0,8},{8,0},{1,9},{9,1},{2,10},{10,2},{3,11},{11,3},{4,12},{12,4},... | collective-permute-start | bytes 393224 | tf_op jit(solution)/shard_map/ppermute | solution.py:109
  62.2 1.3 %collective-permute-done.recv_ref = f32[64,512]{1,0:T(8,128)S(1)} collective-permute-done((f32[64,512]{1,0:T(8,128)S(1)}, f32[64,512]{1,0:T(8,128)S(1)}, u32[]{:S(2)}, u32[]{:S(2)}) %collective-permute-start) | collective-permute-done | bytes 131104 | tf_op jit(solution)/shard_map/ppermute | solution.py:109
  63.5 0.1 rope.2
  63.6 14.1 %all_gather.3.q_ref = bf16[4,64,512]{2,1,0:T(8,128)(2,1)S(1)} all-gather(bf16[1,64,512]{2,1,0:T(8,128)(2,1)S(1)} %rope.2), channel_id=1, replica_groups=mesh['yh'=4,'z'=16,'row'=2,'x'=4,'yl'=2] {'yh'}, dimensions={0}, use_global_device_ids=true | all-gather | bytes 327680 | tf_op jit(solution)/shard_map/all_gather | solution.py:303
  77.7 0.0 collective-permute-done.2.other_ref
  77.7 3.5 %attend.1 = (bf16[4,272,128]{2,1,0:T(8,128)(2,1)S(1)}, bf16[512,4096]{1,0:T(8,128)(2,1)S(1)}) custom-call(s32[128]{0:T(128)} %order_ref.5, bf16[4,64,512]{2,1,0:T(8,128)(2,1)S(1)} %all_gather.3.q_ref, bf16[16,64,256]{2,1,0:T(8,128)(2,1)S(1)} %all_to_all.15.own_ref, bf16[16,64,256]{2,1,0:T(8,128)(2,1)S(1)} %collective-permute-done.2.other_ref, ...), custom_call_target="tpu_custom_call" | custom-call | tf_op jit(solution)/shard_map/attend/pallas_call | solution.py:207
  81.2 12.9 %all_to_all.16.parts_ref = bf16[4,272,128]{2,1,0:T(8,128)(2,1)S(1)} all-to-all(bf16[4,272,128]{2,1,0:T(8,128)(2,1)S(1)} %get-tuple-element.17), channel_id=1, replica_groups=mesh['yh'=4,'z'=16,'row'=2,'x'=4,'yl'=2] {'yh'}, dimensions={0} | all-to-all | bytes 557056 | tf_op jit(solution)/shard_map/all_to_all | solution.py:307
  94.1 1.1 output.1
  95.3 18.4 %all_to_all.17.recv_ref = bf16[16,64,256]{2,1,0:T(8,128)(2,1)S(1)} all-to-all(bf16[16,64,256]{2,1,0:T(8,128)(2,1)S(1)} %output.1), channel_id=1, replica_groups=mesh['yh'=4,'z'=16,'row'=2,'x'=4,'yl'=2] {'row','x','yl'}, dimensions={0} | all-to-all | bytes 1048576 | tf_op jit(solution)/shard_map/all_to_all | solution.py:310
  113.7 0.7 gather.1
  (1 shorter events, 0.0 us)
Async XLA Ops:
  2.6 16.9 %collective-permute-start.1 = (f32[64,256]{1,0:T(8,128)S(1)}, f32[64,256]{1,0:T(8,128)S(1)}, u32[]{:S(2)}, u32[]{:S(2)}) collective-permute-start(f32[64,256]{1,0:T(8,128)S(1)} %get-tuple-element.16), channel_id=1, source_target_pairs={{0,8},{8,0},{1,9},{9,1},{2,10},{10,2},{3,11},{11,3},{4,12},{12,4},... | collective-permute-start | bytes 196616 | tf_op jit(solution)/shard_map/ppermute | solution.py:109
  48.2 29.6 %collective-permute-start.2 = (bf16[16,64,256]{2,1,0:T(8,128)(2,1)S(1)}, bf16[16,64,256]{2,1,0:T(8,128)(2,1)S(1)}, u32[]{:S(2)}, u32[]{:S(2)}) collective-permute-start(bf16[16,64,256]{2,1,0:T(8,128)(2,1)S(1)} %all_to_all.15.own_ref), channel_id=1, source_target_pairs={{0,8},{8,0},{1,9},{9,1},{2,10},{10,2},{3,11},{11,3},{4,12},{12,4},... | collective-permute-start | bytes 1572872 | tf_op jit(solution)/shard_map/ppermute | solution.py:304
  60.3 3.2 %collective-permute-start = (f32[64,512]{1,0:T(8,128)S(1)}, f32[64,512]{1,0:T(8,128)S(1)}, u32[]{:S(2)}, u32[]{:S(2)}) collective-permute-start(f32[64,512]{1,0:T(8,128)S(1)} %get-tuple-element.13), channel_id=1, source_target_pairs={{0,8},{8,0},{1,9},{9,1},{2,10},{10,2},{3,11},{11,3},{4,12},{12,4},... | collective-permute-start | bytes 393224 | tf_op jit(solution)/shard_map/ppermute | solution.py:109
